TPU v7x, 512 devices: a whole 4x8x8 slice. The times are simulated.
512 devices in a mesh: ap: 32 (over x, y), pass: 16 (over z, core).
Axes of the slice: x: 4, y: 8, z: 8, core: 2. Of those that a mesh axis runs over, the one named last changes fastest.
Arguments:
- echo: bfloat16 [16, 256, 2, 3072], P('pass', 'ap'), may hold values from -6 to 6
- chirp: bfloat16 [2, 1024], replicated, may hold values from -0.125 to 0.125
- pair_swap: int32 [16, 8], P('pass'), may hold values from 0 to 1
- range_shift: int32 [16, 8, 2], P('pass'), may hold values from -16 to 16, as said below
- angle_shift: int32 [16, 8, 2, 2], P('pass'), may hold values from -3 to 3, as said below
- range_taps: float32 [8, 2, 8], replicated, may hold values from -2 to 2
- angle_taps: float32 [8, 2, 2, 8], replicated, may hold values from -2 to 2
- phase_rates: float32 [8, 2, 2, 2], replicated, may hold values from -3.140625 to 3.140625
- invert: float32 [2, 64, 32], replicated, may hold values from -1 to 1
- baseline_index: int32 [16], replicated, may hold values from 0 to 31
Outputs:
- tomogram: float32 [16, 64, 32, 1024], P('pass', None, 'ap')
Inputs may be any that keep to these rules, and one draw needn't show every extreme that they name: `range_shift`: both 16 and -16 occur. `angle_shift`: both 3 and -3 occur.
All inputs are finite; a program needn't handle non-finite values.
Results may differ from a plain program's by a relative error of at most 0.0003.
Values sent between devices are 32-bit elements; how exact they have to be, the bound alone decides.
No kernel may reach another device: no remote copies, remote signals or barrier semaphores. Data moves between devices by JAX's collectives and lax.ppermute only.
A program may use at most 64 MiB of HBM per device.

v0:
```python
import math

import jax
import jax.numpy as jnp
from jax import lax
from jax.experimental import pallas as pl
from jax.experimental.pallas import tpu as pltpu
from jax.sharding import PartitionSpec as P

NR = 2048
TAPS = 1024
NS = 3072
HEIGHTS = 64
KT = 8
ORIGIN = KT // 2 - 1
BASES = 32
LEVELS = 8
LOCAL = 3
CROSS = 5
PULSES = 8
N_AP = 32
PASSES = 16
RW = 64
BEAMS = 256
LANES = 128
TILES = 17
WINDOW = TAPS + LANES
SQRT_HALF = math.sqrt(0.5)
F32 = jnp.float32
BF16 = jnp.bfloat16

ROWS = (96, 88, 80, 72, 64)


def iota(shape, dim):
    return lax.broadcasted_iota(jnp.int32, shape, dim)


def sincos(x):
    turns = jnp.floor(x * (2.0 / math.pi) + 0.5)
    quadrant = turns.astype(jnp.int32)
    y = x - turns * 1.5703125
    y = y - turns * 4.837512969970703e-4
    y = y - turns * 7.54978995489188e-8
    y2 = y * y
    s = y * (1.0 + y2 * (-1.6666654611e-1 + y2 * (8.3321608736e-3 + y2 * -1.9515295891e-4)))
    c = 1.0 - 0.5 * y2 + y2 * y2 * (4.166664568298827e-2 + y2 * (-1.388731625493765e-3 + y2 * 2.443315711809948e-5))
    swap = (quadrant & 1) == 1
    cos_abs = jnp.where(swap, s, c)
    sin_abs = jnp.where(swap, c, s)
    cos = jnp.where(((quadrant + 1) & 2) == 2, -cos_abs, cos_abs)
    sin = jnp.where((quadrant & 2) == 2, -sin_abs, sin_abs)
    return cos, sin


def complex_mul(ar, ai, br, bi):
    return ar * br - ai * bi, ar * bi + ai * br


def reverse_bits(value):
    result = 0
    for digit in range(CROSS):
        result = result + (value // 2**digit % 2) * 2 ** (CROSS - 1 - digit)
    return result


def role(swap_ref, level, child):
    flip = swap_ref[0, level]
    return flip if child == 0 else 1 - flip


def step_offset(swap_ref, shift_ref, level, child):
    return shift_ref[0, level, role(swap_ref, level, child)] - ORIGIN


def compress_kernel(
    echo_ref,
    chirp_ref,
    swap_ref,
    range_shift_ref,
    angle_shift_ref,
    range_taps_ref,
    angle_taps_ref,
    rates_ref,
    out_ref,
    echo_rows,
    shifted,
    product,
    images,
):
    position = lax.axis_index("ap")

    offset_above = jnp.int32(0)
    for level in range(LOCAL, LEVELS):
        bit = position // 2 ** (level - LOCAL) % 2
        offset_above = offset_above + jnp.where(
            bit == 1,
            step_offset(swap_ref, range_shift_ref, level, 1),
            step_offset(swap_ref, range_shift_ref, level, 0),
        )
    local_steps = [
        [step_offset(swap_ref, range_shift_ref, level, child) for child in range(2)]
        for level in range(LOCAL)
    ]

    tiles_in = NS // LANES
    tiles_out = TILES + WINDOW // LANES
    lane = iota((2, LANES), 1)
    echo_rows[:, :2] = jnp.zeros((PULSES, 2, 2, LANES), F32)
    echo_rows[:, 2 + tiles_in :] = jnp.zeros((PULSES, 3, 2, LANES), F32)
    for n in range(PULSES):
        total = offset_above
        for level in range(LOCAL):
            total = total + local_steps[level][n >> level & 1]
        whole = total >> 7
        rest = total & (LANES - 1)
        pulse = echo_ref[0, n].astype(F32)
        for t in range(tiles_in):
            echo_rows[n, 2 + t] = pltpu.roll(
                pulse[:, t * LANES : (t + 1) * LANES], (LANES - rest) & (LANES - 1), 1
            )
        keep = lane < LANES - rest
        for t in range(tiles_out):
            index = jnp.clip(t + 2 + whole, 0, tiles_in + 3)
            left = echo_rows[n, index]
            right = echo_rows[n, index + 1]
            shifted[2 * n : 2 * n + 2, t * LANES : (t + 1) * LANES] = jnp.where(keep, left, right)

    signal = shifted[...].astype(BF16)
    windows = jnp.concatenate(
        [signal[:, b * LANES : b * LANES + WINDOW] for b in range(TILES)], axis=0
    )
    bands = []
    row = iota((LANES, LANES), 0)
    column = iota((LANES, LANES), 1)
    for part in range(2):
        previous = jnp.zeros((LANES, LANES), F32)
        pieces = []
        for t in range(WINDOW // LANES):
            if t * LANES < TAPS:
                samples = chirp_ref[part : part + 1, t * LANES : (t + 1) * LANES].astype(F32)
                current = pltpu.roll(
                    jnp.broadcast_to(samples, (LANES, LANES)), 0, 1, stride=1, stride_axis=0
                )
            else:
                current = jnp.zeros((LANES, LANES), F32)
            pieces.append(jnp.where(column >= row, current, previous).astype(BF16))
            previous = current
        bands.append(jnp.concatenate(pieces, axis=1))
    banded = jnp.concatenate(bands, axis=0)
    correlated = lax.dot_general(
        windows, banded, (((1,), (1,)), ((), ())), preferred_element_type=F32
    )
    for part in range(2):
        product[part] = correlated[:, part * LANES : (part + 1) * LANES]

    rows8 = iota((PULSES, LANES), 0)
    lanes8 = iota((PULSES, LANES), 1)

    def row_offset(first_level):
        total = jnp.full((PULSES, LANES), offset_above, jnp.int32)
        for level in range(first_level, LOCAL):
            bit = rows8 >> level & 1
            total = total + jnp.where(bit == 1, local_steps[level][1], local_steps[level][0])
        return total

    cell = row_offset(0) + lanes8
    for b in range(TILES):
        even, odd = (
            [product[part, pl.ds(16 * b + i, PULSES, stride=2), :] for part in range(2)]
            for i in range(2)
        )
        where_r = cell + b * LANES
        inside = (where_r >= 0) & (where_r < NR)
        images[0, 0, b] = jnp.where(inside, even[0] + odd[1], 0.0)
        images[0, 1, b] = jnp.where(inside, odd[0] - even[1], 0.0)
    images[:, :, TILES] = jnp.zeros((2, 2, PULSES, LANES), F32)

    for level in range(LOCAL):
        source, target = level % 2, 1 - level % 2
        beams = 2**level
        in_child = rows8 >> level & 1
        tap_rows = [
            jnp.where(
                in_child == 1,
                range_taps_ref[level, role(swap_ref, level, 1), u],
                range_taps_ref[level, role(swap_ref, level, 0), u],
            )
            for u in range(KT)
        ]
        parity = rows8 & 1
        beam = rows8 % (2 * beams) // 2
        group = rows8 // (2 * beams)
        offset_out = row_offset(level + 1)
        beam_fraction = (rows8 % (2 * beams)).astype(F32) / (2.0 * beams)
        weights = []
        waves = []
        steps = []
        for child in range(2):
            e = role(swap_ref, level, child)
            shift = jnp.where(
                parity == 1, angle_shift_ref[0, level, e, 1], angle_shift_ref[0, level, e, 0]
            )
            columns = [jnp.zeros((PULSES, LANES), F32) for _ in range(beams)]
            for u in range(KT):
                tap = jnp.where(
                    parity == 1, angle_taps_ref[level, e, 1, u], angle_taps_ref[level, e, 0, u]
                )
                picked = jnp.clip(beam + (u - ORIGIN) + shift, 0, beams - 1)
                for k in range(beams):
                    columns[k] = columns[k] + jnp.where(picked == k, tap, 0.0)
            weights.append(columns)
            slope = jnp.where(parity == 1, rates_ref[level, e, 1, 0], rates_ref[level, e, 0, 0])
            bend = jnp.where(parity == 1, rates_ref[level, e, 1, 1], rates_ref[level, e, 0, 1])
            slope = slope * (8.0 / NR)
            cos, sin = sincos(
                slope * (offset_out + lanes8).astype(F32) + 8.0 * (bend * beam_fraction)
            )
            waves.append((cos * SQRT_HALF, sin * SQRT_HALF))
            steps.append(sincos(slope * float(LANES)))
        cell_out = offset_out + lanes8
        for b in range(TILES):
            ranged = []
            for part in range(2):
                here = images[source, part, b]
                there = images[source, part, b + 1]
                total = tap_rows[0] * here
                for u in range(1, KT):
                    moved = jnp.where(
                        lanes8 < LANES - u,
                        pltpu.roll(here, LANES - u, 1),
                        pltpu.roll(there, LANES - u, 1),
                    )
                    total = total + tap_rows[u] * moved
                ranged.append(total)
            out_real = jnp.zeros((PULSES, LANES), F32)
            out_imag = jnp.zeros((PULSES, LANES), F32)
            for child in range(2):
                steered = []
                for part in range(2):
                    total = jnp.zeros((PULSES, LANES), F32)
                    for k in range(beams):
                        spread = jnp.broadcast_to(
                            ranged[part][child * beams + k : child * beams + k + 1], (PULSES, LANES)
                        )
                        for g in range(1, PULSES // (2 * beams)):
                            at = (2 * g + child) * beams + k
                            spread = jnp.where(
                                group == g,
                                jnp.broadcast_to(ranged[part][at : at + 1], (PULSES, LANES)),
                                spread,
                            )
                        total = total + weights[child][k] * spread
                    steered.append(total)
                real, imag = complex_mul(*waves[child], *steered)
                out_real = out_real + real
                out_imag = out_imag + imag
                waves[child] = complex_mul(*waves[child], *steps[child])
            where_r = cell_out + b * LANES
            inside = (where_r >= 0) & (where_r < NR)
            images[target, 0, b] = jnp.where(inside, out_real, 0.0)
            images[target, 1, b] = jnp.where(inside, out_imag, 0.0)

    last = LOCAL % 2
    for block in range(N_AP):
        start = reverse_bits(block) * RW
        t = start // LANES
        for part in range(2):
            if start % LANES == 0:
                value = images[last, part, t]
            else:
                value = jnp.where(
                    lanes8 < RW,
                    pltpu.roll(images[last, part, t], RW, 1),
                    pltpu.roll(images[last, part, t + 1], RW, 1),
                )
            out_ref[block, part * PULSES : (part + 1) * PULSES, :] = value


def merge_kernel(
    blocks_ref,
    swap_ref,
    range_shift_ref,
    angle_shift_ref,
    range_taps_ref,
    angle_taps_ref,
    rates_ref,
    out_ref,
    images,
    final,
):
    position = lax.axis_index("ap")
    base = reverse_bits(position) * RW
    half = LANES

    for child in range(2):
        order = []
        for i in range(N_AP // 2):
            order.append(
                child + 2 * (i >> 3 & 1) + 4 * (i >> 2 & 1) + 8 * (i >> 1 & 1) + 16 * (i & 1)
            )
        for part in range(2):
            stacked = jnp.concatenate(
                [blocks_ref[g, part * PULSES : (part + 1) * PULSES, :] for g in order], axis=0
            )
            images[0, child, part] = stacked.T

    column = iota((1, 2 * half), 1)
    row = iota((half, 2 * half), 0)
    for k in range(CROSS):
        level = LOCAL + k
        beams = 2**level
        rows = ROWS[k]
        source, target = k % 2, 1 - k % 2
        last = k == CROSS - 1
        parity = column & 1
        beam = column % (2 * beams) // 2
        first_row = column // (2 * beams) * beams
        beam_fraction = (column % (2 * beams)).astype(F32) / (2.0 * beams)
        offset = jnp.zeros((1, 2 * half), jnp.int32)
        for later in range(level + 1, LEVELS):
            digit = later - level - 1
            bit = column >> (7 - digit) & 1
            offset = offset + jnp.where(
                bit == 1,
                step_offset(swap_ref, range_shift_ref, later, 1),
                step_offset(swap_ref, range_shift_ref, later, 0),
            )
        cell = iota((8, 2 * half), 0) + (base + offset)
        steered = []
        waves = []
        steps = []
        for child in range(2):
            e = role(swap_ref, level, child)
            parts = []
            for part in range(2):
                total = range_taps_ref[level, e, 0] * images[source, child, part, 0:rows, :]
                for u in range(1, KT):
                    total = total + (
                        range_taps_ref[level, e, u] * images[source, child, part, u : u + rows, :]
                    )
                parts.append(total)
            ranged = jnp.concatenate(parts, axis=0)
            high = ranged.astype(BF16)
            low = (ranged - high.astype(F32)).astype(BF16)

            shift = jnp.where(
                parity == 1, angle_shift_ref[0, level, e, 1], angle_shift_ref[0, level, e, 0]
            )
            weights = jnp.zeros((half, 2 * half), F32)
            for u in range(KT):
                tap = jnp.where(
                    parity == 1, angle_taps_ref[level, e, 1, u], angle_taps_ref[level, e, 0, u]
                )
                picked = first_row + jnp.clip(beam + (u - ORIGIN) + shift, 0, beams - 1)
                weights = weights + jnp.where(row == picked, tap, 0.0)
            weights_high = weights.astype(BF16)
            weights_low = (weights - weights_high.astype(F32)).astype(BF16)
            steered.append(
                jnp.dot(
                    jnp.concatenate([high, low, high], axis=1),
                    jnp.concatenate([weights_high, weights_high, weights_low], axis=0),
                    preferred_element_type=F32,
                )
            )
            slope = jnp.where(parity == 1, rates_ref[level, e, 1, 0], rates_ref[level, e, 0, 0])
            bend = jnp.where(parity == 1, rates_ref[level, e, 1, 1], rates_ref[level, e, 0, 1])
            slope = slope * (8.0 / NR)
            cos, sin = sincos(slope * cell.astype(F32) + 8.0 * (bend * beam_fraction))
            waves.append((cos * SQRT_HALF, sin * SQRT_HALF))
            steps.append(sincos(jnp.broadcast_to(slope * 8.0, (8, 2 * half))))
        for m in range(rows // 8):
            out_real = jnp.zeros((8, 2 * half), F32)
            out_imag = jnp.zeros((8, 2 * half), F32)
            for child in range(2):
                real, imag = complex_mul(
                    *waves[child],
                    steered[child][8 * m : 8 * m + 8],
                    steered[child][rows + 8 * m : rows + 8 * m + 8],
                )
                out_real = out_real + real
                out_imag = out_imag + imag
                waves[child] = complex_mul(*waves[child], *steps[child])
            if last:
                for part, value in enumerate((out_real, out_imag)):
                    for side in range(2):
                        final[part, side, 8 * m : 8 * m + 8] = value[
                            :, side * half : (side + 1) * half
                        ]
            else:
                where_r = cell + 8 * m
                inside = (where_r >= 0) & (where_r < NR)
                for part, value in enumerate((out_real, out_imag)):
                    value = jnp.where(inside, value, 0.0)
                    for child in range(2):
                        images[target, child, part, 8 * m : 8 * m + 8, :] = value[
                            :, child * half : (child + 1) * half
                        ]

    block_of = iota((8, LANES), 1) // 16
    for part in range(2):
        for side in range(2):
            values = [final[part, side, pl.ds(i, 8, stride=8), :] for i in range(8)]
            for d in (4, 2, 1):
                clear = (block_of & d) == 0
                for i in range(8):
                    if i & d == 0:
                        a, b = values[i], values[i | d]
                        values[i] = jnp.where(clear, a, pltpu.roll(b, 16 * d, 1))
                        values[i | d] = jnp.where(clear, pltpu.roll(a, LANES - 16 * d, 1), b)
            for q in range(8):
                out_ref[side * 8 + q, part * 8 : part * 8 + 8, :] = values[q]


def invert_kernel(data_ref, invert_ref, baseline_ref, out_ref):
    column = iota((1, 2 * PASSES), 1)
    wanted = jnp.zeros((1, 2 * PASSES), jnp.int32)
    for p in range(PASSES):
        wanted = jnp.where(column // 2 == p, baseline_ref[p], wanted)
    chosen = (iota((BASES, 2 * PASSES), 0) == wanted).astype(F32)
    highest = lax.Precision.HIGHEST
    steer_real = jnp.dot(invert_ref[0], chosen, precision=highest, preferred_element_type=F32)
    steer_imag = jnp.dot(invert_ref[1], chosen, precision=highest, preferred_element_type=F32)
    imaginary = (iota((HEIGHTS, 2 * PASSES), 1) & 1) == 1
    mixer = jnp.concatenate(
        [
            jnp.where(imaginary, -steer_imag, steer_real),
            jnp.where(imaginary, steer_real, steer_imag),
        ],
        axis=0,
    )
    for i in range(8):
        data = data_ref[pl.ds(i, 2 * PASSES, stride=8), :]
        tomo = jnp.dot(mixer, data, precision=highest, preferred_element_type=F32)
        real, imag = tomo[:HEIGHTS], tomo[HEIGHTS:]
        out_ref[pl.ds(i, HEIGHTS, stride=8), :] = real * real + imag * imag


VMEM = pl.BlockSpec(memory_space=pltpu.VMEM)
SMEM = pl.BlockSpec(memory_space=pltpu.SMEM)


def body(
    echo,
    chirp,
    pair_swap,
    range_shift,
    angle_shift,
    range_taps,
    angle_taps,
    phase_rates,
    invert,
    baseline_index,
):
    tables = (pair_swap, range_shift, angle_shift, range_taps, angle_taps, phase_rates)
    blocks = pl.pallas_call(
        compress_kernel,
        name="compress",
        out_shape=jax.ShapeDtypeStruct((N_AP, 2 * PULSES, LANES), F32),
        in_specs=[VMEM, VMEM] + [SMEM] * 6,
        out_specs=VMEM,
        scratch_shapes=[
            pltpu.VMEM((PULSES, NS // LANES + 5, 2, LANES), F32),
            pltpu.VMEM((2 * PULSES, (TILES + WINDOW // LANES) * LANES), F32),
            pltpu.VMEM((2, TILES * 2 * PULSES, LANES), F32),
            pltpu.VMEM((2, 2, TILES + 1, PULSES, LANES), F32),
        ],
    )(echo, chirp, *tables)
    blocks = lax.all_to_all(blocks, "ap", split_axis=0, concat_axis=0, tiled=True)
    stacks = pl.pallas_call(
        merge_kernel,
        name="merge",
        out_shape=jax.ShapeDtypeStruct((PASSES, 16, LANES), F32),
        in_specs=[VMEM] + [SMEM] * 6,
        out_specs=VMEM,
        scratch_shapes=[
            pltpu.VMEM((2, 2, 2, LANES, LANES), F32),
            pltpu.VMEM((2, 2, RW, LANES), F32),
        ],
    )(blocks, *tables)
    stacks = lax.all_to_all(stacks, "pass", split_axis=0, concat_axis=0, tiled=True)
    power = pl.pallas_call(
        invert_kernel,
        name="invert",
        out_shape=jax.ShapeDtypeStruct((HEIGHTS * 8, LANES), F32),
        in_specs=[VMEM, VMEM, SMEM],
        out_specs=VMEM,
    )(stacks.reshape(PASSES * 16, LANES), invert, baseline_index)
    return power.reshape(1, HEIGHTS, 1, RW * BEAMS // PASSES)


def solution(mesh):
    return jax.shard_map(
        body,
        mesh=mesh,
        in_specs=(
            P("pass", "ap", None, None),
            P(),
            P("pass", None),
            P("pass", None, None),
            P("pass", None, None, None),
            P(),
            P(),
            P(),
            P(),
            P(),
        ),
        out_specs=P("pass", None, "ap", None),
        check_vma=False,
    )
```

profile of v0, /device:TPU:1, one launch (start us, length us, event | category | flops | bytes accessed | tf_op | source)
XLA Modules:
  0.0 59.9 jit_solution(8105840826945359560)
XLA Ops:
  0.0 0.0 copy-start.2
  0.0 1.4 %copy.13.rates_ref = f32[8,2,2,2]{3,2,1,0:T(2,128)} copy(f32[8,2,2,2]{0,3,2,1:T(2,128)} %param.17) | data formatting | bytes 512 | tf_op args[7]
  1.4 0.0 copy-done.2
  1.4 0.0 copy-start.3
  1.4 0.7 %copy.12.angle_shift_ref = s32[1,8,2,2]{3,2,1,0:T(2,128)} copy(s32[1,8,2,2]{1,3,2,0:T(2,128)S(1)} %copy-done.2) | data formatting | bytes 256 | tf_op args[4]
  2.1 0.0 copy-done.3
  2.1 0.7 %copy.11.range_shift_ref = s32[1,8,2]{2,1,0:T(8,128)} copy(s32[1,8,2]{1,2,0:T(2,128)S(1)} %copy-done.3) | data formatting | bytes 128 | tf_op args[3]
  2.8 5.1 %compress.1 = f32[32,16,128]{2,1,0:T(8,128)} custom-call(bf16[1,8,2,3072]{3,2,1,0:T(2,128)(2,1)} %echo_ref.1, bf16[2,1024]{1,0:T(2,128)(2,1)} %chirp_ref.1, s32[1,8]{1,0:T(1,128)} %swap_ref.3, s32[1,8,2]{2,1,0:T(8,128)} %copy.11.range_shift_ref, s32[1,8,2,2]{3,2,1,0:T(2,128)} %copy.12.angle_shift_ref, f32[8,2,8]{2,1,0:T(2,128)} %range_taps_ref.3, ...), custom_call_target="tpu_custom_call" | custom-call | tf_op jit(solution)/shard_map/compress/pallas_call | solution.py:456
  7.8 20.3 %all_to_all.10.blocks_ref = f32[32,16,128]{2,1,0:T(8,128)} all-to-all(f32[32,16,128]{2,1,0:T(8,128)} %compress.1), channel_id=1, replica_groups=mesh['ap'=32,'pass'=16] {'ap'}, dimensions={0} | all-to-all | bytes 524288 | tf_op jit(solution)/shard_map/all_to_all | solution.py:469
  28.1 5.7 %merge.1 = f32[16,16,128]{2,1,0:T(8,128)} custom-call(f32[32,16,128]{2,1,0:T(8,128)} %all_to_all.10.blocks_ref, s32[1,8]{1,0:T(1,128)} %swap_ref.3, s32[1,8,2]{2,1,0:T(8,128)} %copy.11.range_shift_ref, s32[1,8,2,2]{3,2,1,0:T(2,128)} %copy.12.angle_shift_ref, f32[8,2,8]{2,1,0:T(2,128)} %range_taps_ref.3, f32[8,2,2,8]{3,2,1,0:T(2,128)} %angle_taps_ref.3, ...), custom_call_target="tpu_custom_call" | custom-call | tf_op jit(solution)/shard_map/merge/pallas_call | solution.py:470
  33.8 0.0 copy-start.1
  33.8 14.2 %all-to-all-start.1 = ((f32[16,16,128]{2,1,0:T(8,128)}), f32[16,16,128]{2,1,0:T(8,128)S(1)}, u32[]{:S(2)}, u32[]{:S(2)}) async-start(f32[16,16,128]{2,1,0:T(8,128)} %merge.1), calls=%async_computation.1 | async-start | bytes 262144 | tf_op jit(solution)/shard_map/all_to_all | solution.py:481
  48.0 0.0 copy-done.1
  48.0 0.7 %copy.17.invert_ref = f32[2,64,32]{2,1,0:T(8,128)} copy(f32[2,64,32]{1,2,0:T(8,128)S(1)} %copy-done.1) | data formatting | bytes 32768 | tf_op args[8]
  48.7 8.2 %all-to-all-done.1 = f32[16,16,128]{2,1,0:T(8,128)S(1)} async-done(((f32[16,16,128]{2,1,0:T(8,128)}), f32[16,16,128]{2,1,0:T(8,128)S(1)}, u32[]{:S(2)}, u32[]{:S(2)}) %all-to-all-start.1) | async-done | bytes 131104 | tf_op jit(solution)/shard_map/all_to_all | solution.py:481
  56.9 0.0 copy-start
  56.9 0.6 %copy-done = f32[16,16,128]{2,1,0:T(8,128)} copy-done((f32[16,16,128]{2,1,0:T(8,128)}, f32[16,16,128]{2,1,0:T(8,128)S(1)}, u32[]{:S(2)}) %copy-start) | copy-done | bytes 131096
  57.5 2.4 %invert.1 = f32[512,128]{1,0:T(8,128)} custom-call(f32[256,128]{1,0:T(8,128)} %bitcast.2, f32[2,64,32]{2,1,0:T(8,128)} %copy.17.invert_ref, s32[16]{0:T(128)} %baseline_ref.1), custom_call_target="tpu_custom_call" | custom-call | tf_op jit(solution)/shard_map/invert/pallas_call | solution.py:482
Async XLA Ops:
  0.0 1.4 %copy-start.2 = (s32[1,8,2,2]{1,3,2,0:T(2,128)S(1)}, s32[1,8,2,2]{1,3,2,0:T(2,128)}, u32[]{:S(2)}) copy-start(s32[1,8,2,2]{1,3,2,0:T(2,128)} %param.14) | copy-start | bytes 388
  1.4 0.7 %copy-start.3 = (s32[1,8,2]{1,2,0:T(2,128)S(1)}, s32[1,8,2]{1,2,0:T(2,128)}, u32[]{:S(2)}) copy-start(s32[1,8,2]{1,2,0:T(2,128)} %param.13) | copy-start | bytes 196
  33.8 14.2 %copy-start.1 = (f32[2,64,32]{1,2,0:T(8,128)S(1)}, f32[2,64,32]{1,2,0:T(8,128)}, u32[]{:S(2)}) copy-start(f32[2,64,32]{1,2,0:T(8,128)} %param.18) | copy-start | bytes 49156
  33.8 23.1 %all-to-all-start.1 = ((f32[16,16,128]{2,1,0:T(8,128)}), f32[16,16,128]{2,1,0:T(8,128)S(1)}, u32[]{:S(2)}, u32[]{:S(2)}) async-start(f32[16,16,128]{2,1,0:T(8,128)} %merge.1), calls=%async_computation.1 | async-start | bytes 262144 | tf_op jit(solution)/shard_map/all_to_all | solution.py:481
  56.9 0.6 %copy-start = (f32[16,16,128]{2,1,0:T(8,128)}, f32[16,16,128]{2,1,0:T(8,128)S(1)}, u32[]{:S(2)}) copy-start(f32[16,16,128]{2,1,0:T(8,128)S(1)} %all-to-all-done.1) | copy-start | bytes 393220
where the time goes:
time: 60.4 us; the launch traced here: 59.9 us
  blocking collectives  20.3 us (34%)
  starting transfers between devices  14.2 us (24%)
  Pallas kernels  13.1 us (22%)
  waiting for transfers between devices  8.17 us (14%)
  local copies, waits for them, and re-layouts  4.1 us (7%)
    all_to_all x1, blocking collectives, body(): lax.all_to_all(blocks, 'ap', split_axis=0, concat_axis=0, tiled=True)  20.3 us
    all_to_all x1, starting transfers between devices, body(): lax.all_to_all(stacks, 'pass', split_axis=0, concat_axis=0, tiled=True)  14.2 us
    all_to_all x1, waiting for transfers between devices, body(): lax.all_to_all(stacks, 'pass', split_axis=0, concat_axis=0, tiled=True)  8.17 us
    pallas_call x1, Pallas kernels, body(): pl.pallas_call(merge_kernel, name='merge', out_shape=jax.ShapeDtypeStruct...  5.68 us
    pallas_call x1, Pallas kernels, body(): pl.pallas_call(compress_kernel, name='compress', out_shape=jax.ShapeDtype...  5.08 us
    unnamed x12, local copies, waits for them, and re-layouts  4.1 us
    pallas_call x1, Pallas kernels, body(): pl.pallas_call(invert_kernel, name='invert', out_shape=jax.ShapeDtypeStru...  2.37 us
  transfers between devices with their start and end apart: 1, of which 1 were waited for; matrix products, arithmetic and copies ran while one was open for 1% of the time, Pallas kernels for 0%

commit v1 on v0

v1 whole, which is shorter than its diff:
```python
import math

import jax
import jax.numpy as jnp
from jax import lax
from jax.experimental import pallas as pl
from jax.experimental.pallas import tpu as pltpu
from jax.sharding import PartitionSpec as P

NR = 2048
TAPS = 1024
NS = 3072
HEIGHTS = 64
KT = 8
ORIGIN = KT // 2 - 1
BASES = 32
LEVELS = 8
LOCAL = 3
CROSS = 5
PULSES = 8
N_AP = 32
PASSES = 16
RW = 64
BEAMS = 256
LANES = 128
TILES = 17
BLOCKS = NR // LANES
FRAME_ROWS = 24
WINDOW = TAPS + LANES
SQRT_HALF = math.sqrt(0.5)
F32 = jnp.float32
BF16 = jnp.bfloat16

ROWS = (96, 88, 80, 72, 64)


def iota(shape, dim):
    return lax.broadcasted_iota(jnp.int32, shape, dim)


def sincos(x):
    turns = jnp.floor(x * (2.0 / math.pi) + 0.5)
    quadrant = turns.astype(jnp.int32)
    y = x - turns * 1.5703125
    y = y - turns * 4.837512969970703e-4
    y = y - turns * 7.54978995489188e-8
    y2 = y * y
    s = y * (1.0 + y2 * (-1.6666654611e-1 + y2 * (8.3321608736e-3 + y2 * -1.9515295891e-4)))
    c = 1.0 - 0.5 * y2 + y2 * y2 * (4.166664568298827e-2 + y2 * (-1.388731625493765e-3 + y2 * 2.443315711809948e-5))
    swap = (quadrant & 1) == 1
    cos_abs = jnp.where(swap, s, c)
    sin_abs = jnp.where(swap, c, s)
    cos = jnp.where(((quadrant + 1) & 2) == 2, -cos_abs, cos_abs)
    sin = jnp.where((quadrant & 2) == 2, -sin_abs, sin_abs)
    return cos, sin


def complex_mul(ar, ai, br, bi):
    return ar * br - ai * bi, ar * bi + ai * br


def reverse_bits(value):
    result = 0
    for digit in range(CROSS):
        result = result + (value // 2**digit % 2) * 2 ** (CROSS - 1 - digit)
    return result


def role(tables, level, child):
    flip = tables[0][0, level]
    return flip if child == 0 else 1 - flip


def step_offset(tables, level, child):
    return tables[1][0, role(tables, level, child), level] - ORIGIN


def slope_and_bend(tables, level, e, parity):
    rates = tables[5]
    slope = jnp.where(parity == 1, rates[e, 1, 0, level], rates[e, 0, 0, level])
    bend = jnp.where(parity == 1, rates[e, 1, 1, level], rates[e, 0, 1, level])
    return slope * (8.0 / NR), 8.0 * bend


def split(value):
    high = value.astype(BF16).astype(F32)
    return high, value - high


def start_copies(sources, targets, arrived):
    copies = [
        pltpu.make_async_copy(source, target, arrived.at[i])
        for i, (source, target) in enumerate(zip(sources, targets))
    ]
    for copy in copies:
        copy.start()
    return copies


def compress_kernel(
    echo_ref,
    chirp_ref,
    swap_ref,
    range_shift_ref,
    angle_shift_ref,
    range_taps_ref,
    angle_taps_ref,
    rates_ref,
    out_ref,
    echo,
    chirp,
    echo_rows,
    product,
    shifting,
    framed,
    images,
    *scalars,
):
    *tables, arrived = scalars
    fetch_chirp = pltpu.make_async_copy(chirp_ref, chirp, arrived.at[len(tables)])
    fetch_chirp.start()
    fetch = pltpu.make_async_copy(echo_ref.at[0], echo, arrived.at[len(tables) + 1])
    fetch.start()
    fetch_tables = start_copies(
        (
            swap_ref,
            range_shift_ref,
            angle_shift_ref,
            range_taps_ref,
            angle_taps_ref,
            rates_ref,
        ),
        tables,
        arrived,
    )
    _, _, angle_shift_ref, range_taps_ref, angle_taps_ref, _ = tables
    rows8 = iota((PULSES, LANES), 0)
    lanes8 = iota((PULSES, LANES), 1)

    fetch_chirp.wait()
    bands = []
    row = iota((LANES, LANES), 0)
    column = iota((LANES, LANES), 1)
    for part in range(2):
        previous = jnp.zeros((LANES, LANES), F32)
        pieces = []
        for t in range(WINDOW // LANES):
            if t * LANES < TAPS:
                samples = chirp[part : part + 1, t * LANES : (t + 1) * LANES].astype(F32)
                current = pltpu.roll(
                    jnp.broadcast_to(samples, (LANES, LANES)), 0, 1, stride=1, stride_axis=0
                )
            else:
                current = jnp.zeros((LANES, LANES), F32)
            pieces.append(jnp.where(column >= row, current, previous).astype(BF16))
            previous = current
        bands.append(jnp.concatenate(pieces, axis=1))
    banded = jnp.concatenate(bands, axis=0)
    for copy in fetch_tables:
        copy.wait()

    position = lax.axis_index("ap")
    offset_above = jnp.int32(0)
    for level in range(LOCAL, LEVELS):
        bit = position // 2 ** (level - LOCAL) % 2
        offset_above = offset_above + jnp.where(
            bit == 1, step_offset(tables, level, 1), step_offset(tables, level, 0)
        )
    local_steps = [
        [step_offset(tables, level, child) for child in range(2)] for level in range(LOCAL)
    ]
    shifting[:, :8] = jnp.zeros((2 * PULSES, 8, LANES), F32)
    shifting[:, 8 + BLOCKS :] = jnp.zeros((2 * PULSES, 16, LANES), F32)

    fetch.wait()
    for n in range(PULSES):
        echo_rows[2 * n : 2 * n + 2, :] = echo[n].astype(F32)
    signal = echo_rows[...].astype(BF16)
    windows = jnp.concatenate(
        [signal[:, b * LANES : b * LANES + WINDOW] for b in range(BLOCKS)], axis=0
    )
    correlated = lax.dot_general(
        windows, banded, (((1,), (1,)), ((), ())), preferred_element_type=F32
    )
    for part in range(2):
        product[part] = correlated[:, part * LANES : (part + 1) * LANES]

    for n in range(PULSES):
        total = offset_above
        for level in range(LOCAL):
            total = total + local_steps[level][n >> level & 1]
        whole = total >> 7
        rest = total & (LANES - 1)
        even, odd = (
            [product[part, pl.ds(2 * n + i, BLOCKS, stride=16), :] for part in range(2)]
            for i in range(2)
        )
        keep = iota((FRAME_ROWS, LANES), 1) < LANES - rest
        for part, value in enumerate((even[0] + odd[1], odd[0] - even[1])):
            i = 2 * n + part
            shifting[i, 8 : 8 + BLOCKS] = pltpu.roll(value, (LANES - rest) & (LANES - 1), 1)
            left = shifting[i, pl.ds(8 + whole, FRAME_ROWS), :]
            right = shifting[i, pl.ds(9 + whole, FRAME_ROWS), :]
            framed[i * FRAME_ROWS : (i + 1) * FRAME_ROWS] = jnp.where(keep, left, right)

    def load(level, part, b):
        if level == 0:
            return framed[pl.ds(part * FRAME_ROWS + b, PULSES, stride=2 * FRAME_ROWS), :]
        return images[level % 2, part, b]

    for level in range(LOCAL):
        beams = 2**level
        roles = [role(tables, level, child) for child in range(2)]
        in_child = rows8 >> level & 1
        tap_rows = [
            jnp.where(
                in_child == 1,
                range_taps_ref[level, roles[1], u],
                range_taps_ref[level, roles[0], u],
            )
            for u in range(KT)
        ]

        row16 = iota((2 * PULSES, LANES), 0)
        lane16 = iota((2 * PULSES, LANES), 1)
        of_child = row16 >> 3
        row_out = row16 & 7
        parity16 = row16 & 1

        def of_row(pick):
            return jnp.where(
                of_child == 1,
                jnp.where(parity16 == 1, pick(roles[1], 1), pick(roles[1], 0)),
                jnp.where(parity16 == 1, pick(roles[0], 1), pick(roles[0], 0)),
            )

        shift = of_row(lambda e, h: angle_shift_ref[0, e, h, level])
        beam = row_out % (2 * beams) // 2
        first = (row_out // (2 * beams) * 2 + of_child) * beams
        weights = jnp.zeros((2 * PULSES, LANES), F32)
        for u in range(KT):
            picked = first + jnp.clip(beam + (u - ORIGIN) + shift, 0, beams - 1)
            tap = of_row(lambda e, h: angle_taps_ref[level, e, h, u])
            weights = weights + jnp.where((lane16 & 7) == picked, tap, 0.0)
        high, low = split(weights)
        piece = lane16 >> 3
        left_side = jnp.where(piece < 2, high, jnp.where(piece == 2, low, 0.0)).astype(BF16)[:, :32]

        offset_out = jnp.full((PULSES, LANES), offset_above, jnp.int32)
        for later in range(level + 1, LOCAL):
            offset_out = offset_out + jnp.where(
                (rows8 >> later & 1) == 1, local_steps[later][1], local_steps[later][0]
            )
        cell_out = offset_out + lanes8
        beam_fraction = (rows8 % (2 * beams)).astype(F32) / (2.0 * beams)
        waves = []
        steps = []
        for child in range(2):
            slope, bend = slope_and_bend(tables, level, roles[child], rows8 & 1)
            cos, sin = sincos(slope * cell_out.astype(F32) + bend * beam_fraction)
            waves.append((cos * SQRT_HALF, sin * SQRT_HALF))
            steps.append(sincos(slope * float(LANES)))

        def rolls(b):
            found = []
            for part in range(2):
                value = load(level, part, b)
                found.append([value] + [pltpu.roll(value, LANES - u, 1) for u in range(1, KT)])
            return found

        here = rolls(0)
        for b in range(TILES):
            there = rolls(b + 1) if b + 1 < TILES else here
            pieces = []
            for part in range(2):
                total = tap_rows[0] * here[part][0]
                for u in range(1, KT):
                    moved = jnp.where(lanes8 < LANES - u, here[part][u], there[part][u])
                    total = total + tap_rows[u] * moved
                high, low = split(total)
                pieces.append(
                    jnp.concatenate([high, low, high, jnp.zeros((PULSES, LANES), F32)], axis=0)
                )
            right_side = jnp.concatenate(pieces, axis=1).astype(BF16)
            steered = jnp.dot(left_side, right_side, preferred_element_type=F32)
            out_real = jnp.zeros((PULSES, LANES), F32)
            out_imag = jnp.zeros((PULSES, LANES), F32)
            for child in range(2):
                rows = steered[child * PULSES : (child + 1) * PULSES]
                real, imag = complex_mul(*waves[child], rows[:, :LANES], rows[:, LANES:])
                out_real = out_real + real
                out_imag = out_imag + imag
                waves[child] = complex_mul(*waves[child], *steps[child])
            where_r = cell_out + b * LANES
            inside = (where_r >= 0) & (where_r < NR)
            images[(level + 1) % 2, 0, b] = jnp.where(inside, out_real, 0.0)
            images[(level + 1) % 2, 1, b] = jnp.where(inside, out_imag, 0.0)
            here = there

    last = LOCAL % 2
    for block in range(N_AP):
        start = reverse_bits(block) * RW
        t = start // LANES
        for part in range(2):
            if start % LANES == 0:
                value = images[last, part, t]
            else:
                value = jnp.where(
                    lanes8 < RW,
                    pltpu.roll(images[last, part, t], RW, 1),
                    pltpu.roll(images[last, part, t + 1], RW, 1),
                )
            out_ref[block, part * PULSES : (part + 1) * PULSES, :] = value


def column_offset(tables, level, column):
    offset = jnp.zeros_like(column)
    for later in range(level + 1, LEVELS):
        bit = column >> (7 - (later - level - 1)) & 1
        offset = offset + jnp.where(
            bit == 1, step_offset(tables, later, 1), step_offset(tables, later, 0)
        )
    return offset


def tables_kernel(
    swap_ref,
    range_shift_ref,
    angle_shift_ref,
    range_taps_ref,
    angle_taps_ref,
    rates_ref,
    invert_ref,
    baseline_ref,
    weights_ref,
    waves_ref,
    taps_ref,
    mixer_ref,
    invert,
    baseline,
    *scalars,
):
    *tables, arrived = scalars
    for copy in start_copies(
        (
            swap_ref,
            range_shift_ref,
            angle_shift_ref,
            range_taps_ref,
            angle_taps_ref,
            rates_ref,
            invert_ref,
            baseline_ref,
        ),
        (*tables, invert, baseline),
        arrived,
    ):
        copy.wait()
    _, _, angle_shift_ref, range_taps_ref, angle_taps_ref, _ = tables
    position = lax.axis_index("ap")
    base = reverse_bits(position) * RW
    column = iota((1, 2 * LANES), 1)
    row = iota((LANES, 2 * LANES), 0)
    parity = column & 1
    for k in range(CROSS):
        level = LOCAL + k
        beams = 2**level
        beam = column % (2 * beams) // 2
        first_row = column // (2 * beams) * beams
        beam_fraction = (column % (2 * beams)).astype(F32) / (2.0 * beams)
        cell = iota((8, 2 * LANES), 0) + (base + column_offset(tables, level, column))
        for child in range(2):
            e = role(tables, level, child)
            shift = jnp.where(
                parity == 1, angle_shift_ref[0, e, 1, level], angle_shift_ref[0, e, 0, level]
            )
            weights = jnp.zeros((LANES, 2 * LANES), F32)
            for u in range(KT):
                tap = jnp.where(
                    parity == 1, angle_taps_ref[level, e, 1, u], angle_taps_ref[level, e, 0, u]
                )
                picked = first_row + jnp.clip(beam + (u - ORIGIN) + shift, 0, beams - 1)
                weights = weights + jnp.where(row == picked, tap, 0.0)
            high, low = split(weights)
            at = 2 * k + child
            weights_ref[at, :LANES] = high.astype(BF16)
            weights_ref[at, LANES:] = low.astype(BF16)
            slope, bend = slope_and_bend(tables, level, e, parity)
            cos, sin = sincos(slope * cell.astype(F32) + bend * beam_fraction)
            waves_ref[at, 0] = cos * SQRT_HALF
            waves_ref[at, 1] = sin * SQRT_HALF
            cos, sin = sincos(jnp.broadcast_to(slope * 8.0, (8, 2 * LANES)))
            waves_ref[at, 2] = cos
            waves_ref[at, 3] = sin
            waves_ref[at, 4] = cell.astype(F32)
            for u in range(KT):
                taps_ref[at, u] = jnp.full((8, LANES), range_taps_ref[level, e, u], F32)

    lane = iota((1, LANES), 1)
    wanted = jnp.zeros((1, LANES), jnp.int32)
    for p in range(PASSES):
        wanted = jnp.where(lane % (2 * PASSES) // 2 == p, baseline[p], wanted)
    chosen = (iota((BASES, LANES), 0) == wanted).astype(F32)
    steer = [
        lax.dot_general(
            invert[part],
            chosen,
            (((0,), (0,)), ((), ())),
            precision=lax.Precision.HIGHEST,
            preferred_element_type=F32,
        )
        for part in range(2)
    ]
    imaginary = (lane & 1) == 1
    high, low = split(
        jnp.concatenate(
            [jnp.where(imaginary, -steer[1], steer[0]), jnp.where(imaginary, steer[0], steer[1])],
            axis=0,
        )
    )
    piece = lane // (2 * PASSES)
    mixer_ref[...] = jnp.where(piece < 2, high, jnp.where(piece == 2, low, 0.0)).astype(BF16)


def merge_kernel(
    blocks_ref,
    weights_ref,
    waves_ref,
    taps_ref,
    out_ref,
    blocks,
    weights,
    waves,
    taps,
    images,
    final,
    arrived,
):
    fetches = [pltpu.make_async_copy(blocks_ref, blocks, arrived.at[CROSS])]
    fetches += [
        pltpu.make_async_copy(
            weights_ref.at[pl.ds(2 * k, 2)], weights.at[pl.ds(2 * k, 2)], arrived.at[k]
        )
        for k in range(CROSS)
    ]
    fetches.append(pltpu.make_async_copy(waves_ref, waves, arrived.at[CROSS + 1]))
    fetches.append(pltpu.make_async_copy(taps_ref, taps, arrived.at[CROSS + 2]))
    for fetch in fetches:
        fetch.start()
    fetches[0].wait()
    for child in range(2):
        order = []
        for i in range(N_AP // 2):
            order.append(
                child + 2 * (i >> 3 & 1) + 4 * (i >> 2 & 1) + 8 * (i >> 1 & 1) + 16 * (i & 1)
            )
        for part in range(2):
            stacked = jnp.concatenate(
                [blocks[g, part * PULSES : (part + 1) * PULSES, :] for g in order], axis=0
            )
            images[0, child, part] = stacked.T

    fetches[CROSS + 1].wait()
    fetches[CROSS + 2].wait()
    for k in range(CROSS):
        rows = ROWS[k]
        source, target = k % 2, 1 - k % 2
        last = k == CROSS - 1
        fetches[1 + k].wait()
        steered = []
        for child in range(2):
            tap = [
                jnp.concatenate([taps[2 * k + child, u]] * (rows // 8), axis=0) for u in range(KT)
            ]
            parts = []
            for part in range(2):
                total = tap[0] * images[source, child, part, 0:rows, :]
                for u in range(1, KT):
                    total = total + tap[u] * images[source, child, part, u : u + rows, :]
                parts.append(total)
            ranged = jnp.concatenate(parts, axis=0)
            high = ranged.astype(BF16)
            low = (ranged - high.astype(F32)).astype(BF16)
            matrix = weights[2 * k + child]
            steered.append(
                jnp.dot(
                    jnp.concatenate([high, low, high], axis=1),
                    jnp.concatenate([matrix[:LANES], matrix[:LANES], matrix[LANES:]], axis=0),
                    preferred_element_type=F32,
                )
            )
        turning = [(waves[2 * k + child, 0], waves[2 * k + child, 1]) for child in range(2)]
        steps = [(waves[2 * k + child, 2], waves[2 * k + child, 3]) for child in range(2)]
        for m in range(rows // 8):
            out_real = jnp.zeros((8, 2 * LANES), F32)
            out_imag = jnp.zeros((8, 2 * LANES), F32)
            for child in range(2):
                real, imag = complex_mul(
                    *turning[child],
                    steered[child][8 * m : 8 * m + 8],
                    steered[child][rows + 8 * m : rows + 8 * m + 8],
                )
                out_real = out_real + real
                out_imag = out_imag + imag
                turning[child] = complex_mul(*turning[child], *steps[child])
            if not last:
                where_r = waves[2 * k, 4] + float(8 * m)
                inside = (where_r >= 0) & (where_r < NR)
                out_real = jnp.where(inside, out_real, 0.0)
                out_imag = jnp.where(inside, out_imag, 0.0)
            for part, value in enumerate((out_real, out_imag)):
                for side in range(2):
                    piece = value[:, side * LANES : (side + 1) * LANES]
                    if last:
                        final[part, side, 8 * m : 8 * m + 8] = piece
                    else:
                        images[target, side, part, 8 * m : 8 * m + 8, :] = piece

    block_of = iota((8, LANES), 1) // 16
    for part in range(2):
        for side in range(2):
            values = [final[part, side, pl.ds(i, 8, stride=8), :] for i in range(8)]
            for d in (4, 2, 1):
                clear = (block_of & d) == 0
                for i in range(8):
                    if i & d == 0:
                        a, b = values[i], values[i | d]
                        values[i] = jnp.where(clear, a, pltpu.roll(b, 16 * d, 1))
                        values[i | d] = jnp.where(clear, pltpu.roll(a, LANES - 16 * d, 1), b)
            for q in range(8):
                out_ref[side * 8 + q, part * 8 : part * 8 + 8, :] = values[q]


def invert_kernel(data_ref, mixer_ref, out_ref, data, arrived):
    fetch = pltpu.make_async_copy(data_ref, data, arrived)
    fetch.start()
    mixer = mixer_ref[...]
    fetch.wait()
    for i in range(8):
        high, low = split(data[pl.ds(i, 2 * PASSES, stride=8), :])
        right_side = jnp.concatenate([high, low, high, jnp.zeros_like(high)], axis=0)
        tomo = jnp.dot(mixer, right_side.astype(BF16), preferred_element_type=F32)
        real, imag = tomo[:HEIGHTS], tomo[HEIGHTS:]
        out_ref[pl.ds(i, HEIGHTS, stride=8), :] = real * real + imag * imag


VMEM = pl.BlockSpec(memory_space=pltpu.VMEM)
ANY = pl.BlockSpec(memory_space=pl.ANY)
HBM = pl.BlockSpec(memory_space=pltpu.HBM)
LIMIT = 16 << 20


def in_hbm(array):
    return pltpu.with_memory_space_constraint(array, pltpu.HBM)


def body(
    echo,
    chirp,
    pair_swap,
    range_shift,
    angle_shift,
    range_taps,
    angle_taps,
    phase_rates,
    invert,
    baseline_index,
):
    tables = (
        pair_swap,
        jnp.transpose(range_shift, (0, 2, 1)),
        jnp.transpose(angle_shift, (0, 2, 3, 1)),
        range_taps,
        angle_taps,
        jnp.transpose(phase_rates, (1, 2, 3, 0)),
    )
    tables = [in_hbm(table) for table in tables]
    held = [pltpu.SMEM(table.shape, table.dtype) for table in tables]
    params = pltpu.CompilerParams(vmem_limit_bytes=LIMIT)
    blocks = pl.pallas_call(
        compress_kernel,
        name="compress",
        out_shape=jax.ShapeDtypeStruct((N_AP, 2 * PULSES, LANES), F32),
        in_specs=[HBM] * 8,
        out_specs=VMEM,
        scratch_shapes=[
            pltpu.VMEM((PULSES, 2, NS), BF16),
            pltpu.VMEM((2, TAPS), BF16),
            pltpu.VMEM((2 * PULSES, NS), F32),
            pltpu.VMEM((2, 2 * PULSES * BLOCKS, LANES), F32),
            pltpu.VMEM((2 * PULSES, 24 + BLOCKS, LANES), F32),
            pltpu.VMEM((2 * PULSES * FRAME_ROWS, LANES), F32),
            pltpu.VMEM((2, 2, TILES, PULSES, LANES), F32),
            *held,
            pltpu.SemaphoreType.DMA((8,)),
        ],
        compiler_params=params,
        cost_estimate=pl.CostEstimate(flops=10**8, bytes_accessed=10**6, transcendentals=0),
    )(in_hbm(echo), in_hbm(chirp), *tables)
    weights, waves, taps, mixer = pl.pallas_call(
        tables_kernel,
        name="tables",
        out_shape=(
            jax.ShapeDtypeStruct((2 * CROSS, 2 * LANES, 2 * LANES), BF16),
            jax.ShapeDtypeStruct((2 * CROSS, 5, 8, 2 * LANES), F32),
            jax.ShapeDtypeStruct((2 * CROSS, KT, 8, LANES), F32),
            jax.ShapeDtypeStruct((2 * HEIGHTS, LANES), BF16),
        ),
        in_specs=[HBM] * 8,
        out_specs=(VMEM,) * 4,
        scratch_shapes=[
            pltpu.VMEM((2, BASES, HEIGHTS), F32),
            pltpu.SMEM((PASSES,), jnp.int32),
            *held,
            pltpu.SemaphoreType.DMA((8,)),
        ],
        compiler_params=params,
        cost_estimate=pl.CostEstimate(flops=10**8, bytes_accessed=10**6, transcendentals=0),
    )(*tables, in_hbm(jnp.transpose(invert, (0, 2, 1))), in_hbm(baseline_index))
    blocks = lax.all_to_all(blocks, "ap", split_axis=0, concat_axis=0, tiled=True)
    stacks = pl.pallas_call(
        merge_kernel,
        name="merge",
        out_shape=jax.ShapeDtypeStruct((PASSES, 16, LANES), F32),
        in_specs=[ANY] * 4,
        out_specs=VMEM,
        scratch_shapes=[
            pltpu.VMEM((N_AP, 2 * PULSES, LANES), F32),
            pltpu.VMEM((2 * CROSS, 2 * LANES, 2 * LANES), BF16),
            pltpu.VMEM((2 * CROSS, 5, 8, 2 * LANES), F32),
            pltpu.VMEM((2 * CROSS, KT, 8, LANES), F32),
            pltpu.VMEM((2, 2, 2, LANES, LANES), F32),
            pltpu.VMEM((2, 2, RW, LANES), F32),
            pltpu.SemaphoreType.DMA((CROSS + 3,)),
        ],
        compiler_params=params,
        cost_estimate=pl.CostEstimate(flops=10**8, bytes_accessed=10**6, transcendentals=0),
    )(blocks, weights, waves, taps)
    stacks = lax.all_to_all(stacks, "pass", split_axis=0, concat_axis=0, tiled=True)
    power = pl.pallas_call(
        invert_kernel,
        name="invert",
        out_shape=jax.ShapeDtypeStruct((HEIGHTS * 8, LANES), F32),
        in_specs=[ANY, VMEM],
        out_specs=VMEM,
        scratch_shapes=[pltpu.VMEM((PASSES * 16, LANES), F32), pltpu.SemaphoreType.DMA],
        compiler_params=params,
        cost_estimate=pl.CostEstimate(flops=10**8, bytes_accessed=10**6, transcendentals=0),
    )(stacks.reshape(PASSES * 16, LANES), mixer)
    return power.reshape(1, HEIGHTS, 1, RW * BEAMS // PASSES)


def solution(mesh):
    return jax.shard_map(
        body,
        mesh=mesh,
        in_specs=(
            P("pass", "ap", None, None),
            P(),
            P("pass", None),
            P("pass", None, None),
            P("pass", None, None, None),
            P(),
            P(),
            P(),
            P(),
            P(),
        ),
        out_specs=P("pass", None, "ap", None),
        check_vma=False,
    )
```

time: 60.4 us -> 50.8 us (0.84)
  local copies, waits for them, and re-layouts: 4.1 us -> 0 us
  starting transfers between devices: 14.2 us -> 10.5 us
  waiting for transfers between devices: 8.17 us -> 5.46 us
  blocking collectives: 20.3 us -> 22.7 us
  Pallas kernels: 13.1 us -> 11.7 us
    pallas_call x0 -> x1, Pallas kernels: none -> 4.21 us  [body(): pl.pallas_call(tables_kernel, name='tables', out_shape=(jax.ShapeDtypeStr...]
    unnamed x12 -> x0, local copies, waits for them, and re-layouts: 4.1 us -> none
    all_to_all x1, starting transfers between devices: 14.2 us -> 10.5 us  [body(): lax.all_to_all(blocks, 'ap', split_axis=0, concat_axis=0, tiled=True)]
    pallas_call x1, Pallas kernels: 5.68 us -> 2.44 us  [body(): pl.pallas_call(merge_kernel, name='merge', out_shape=jax.ShapeDtypeStruct...]
    all_to_all x1, waiting for transfers between devices: 8.17 us -> 5.46 us  [body(): lax.all_to_all(blocks, 'ap', split_axis=0, concat_axis=0, tiled=True)]
    all_to_all x1, blocking collectives: 20.3 us -> 22.7 us  [body(): lax.all_to_all(stacks, 'pass', split_axis=0, concat_axis=0, tiled=True)]
    pallas_call x1, Pallas kernels: 2.37 us -> 1.07 us  [body(): pl.pallas_call(invert_kernel, name='invert', out_shape=jax.ShapeDtypeStru...]
    pallas_call x1, Pallas kernels: 5.08 us -> 3.96 us  [body(): pl.pallas_call(compress_kernel, name='compress', out_shape=jax.ShapeDtype...]
  transfers between devices with their start and end apart: 1 -> 1, of which waited for: 1 -> 1; matrix products, arithmetic and copies ran while one was open for 1% -> 0% of each run, Pallas kernels for 0% -> 8%
where the time goes in v1:
time: 50.8 us; the launch traced here: 50.4 us
  blocking collectives  22.7 us (45%)
  Pallas kernels  11.7 us (23%)
  starting transfers between devices  10.5 us (21%)
  waiting for transfers between devices  5.46 us (11%)
    all_to_all x1, blocking collectives, body(): lax.all_to_all(stacks, 'pass', split_axis=0, concat_axis=0, tiled=True)  22.7 us
    all_to_all x1, starting transfers between devices, body(): lax.all_to_all(blocks, 'ap', split_axis=0, concat_axis=0, tiled=True)  10.5 us
    all_to_all x1, waiting for transfers between devices, body(): lax.all_to_all(blocks, 'ap', split_axis=0, concat_axis=0, tiled=True)  5.46 us
    pallas_call x1, Pallas kernels, body(): pl.pallas_call(tables_kernel, name='tables', out_shape=(jax.ShapeDtypeStr...  4.21 us
    pallas_call x1, Pallas kernels, body(): pl.pallas_call(compress_kernel, name='compress', out_shape=jax.ShapeDtype...  3.96 us
    pallas_call x1, Pallas kernels, body(): pl.pallas_call(merge_kernel, name='merge', out_shape=jax.ShapeDtypeStruct...  2.44 us
    pallas_call x1, Pallas kernels, body(): pl.pallas_call(invert_kernel, name='invert', out_shape=jax.ShapeDtypeStru...  1.07 us
  transfers between devices with their start and end apart: 1, of which 1 were waited for; matrix products, arithmetic and copies ran while one was open for 0% of the time, Pallas kernels for 8%

profile of v1, /device:TPU:1, one launch (start us, length us, event | category | flops | bytes accessed | tf_op | source)
XLA Modules:
  0.0 50.4 jit_solution(17264174591742981588)
XLA Ops:
  0.0 4.0 %compress.1 = f32[32,16,128]{2,1,0:T(8,128)} custom-call(bf16[1,8,2,3072]{3,2,1,0:T(2,128)(2,1)} %echo_ref.1, bf16[2,1024]{1,0:T(2,128)(2,1)} %chirp_ref.1, s32[1,8]{1,0:T(1,128)} %swap_ref.3, s32[1,2,8]{2,1,0:T(2,128)} %bitcast.11, s32[1,2,2,8]{3,2,1,0:T(2,128)} %bitcast.9, f32[8,2,8]{2,1,0:T(2,128)} %range_taps_ref.3, f32[8,2,2,8]{3,2,1,0:T(2,128)} %angle_taps_ref.3, ...), custom_call_target="tpu_custom_call" | custom-call | flops 100000000 | bytes 1000000 | tf_op jit(solution)/shard_map/compress/pallas_call | solution.py:580
  4.0 10.5 %all-to-all-start = ((f32[32,16,128]{2,1,0:T(8,128)}), f32[32,16,128]{2,1,0:T(8,128)S(1)}, u32[]{:S(2)}, u32[]{:S(2)}) async-start(f32[32,16,128]{2,1,0:T(8,128)} %compress.1), calls=%async_computation | async-start | bytes 524288 | tf_op jit(solution)/shard_map/all_to_all | solution.py:620
  14.5 4.2 %tables.1 = (bf16[10,256,256]{2,1,0:T(8,128)(2,1)S(1)}, f32[10,5,8,256]{3,2,1,0:T(8,128)S(1)}, f32[10,8,8,128]{3,2,1,0:T(8,128)S(1)}, bf16[128,128]{1,0:T(8,128)(2,1)S(1)}) custom-call(s32[1,8]{1,0:T(1,128)} %swap_ref.3, s32[1,2,8]{2,1,0:T(2,128)} %bitcast.12, s32[1,2,2,8]{3,2,1,0:T(2,128)} %bitcast.10, f32[8,2,8]{2,1,0:T(2,128)} %range_taps_ref.3, ...), custom_call_target="tpu_custom_call" | custom-call | flops 100000000 | bytes 1000000 | tf_op jit(solution)/shard_map/tables/pallas_call | solution.py:600
  18.7 5.5 %all-to-all-done.blocks_ref = f32[32,16,128]{2,1,0:T(8,128)S(1)} async-done(((f32[32,16,128]{2,1,0:T(8,128)}), f32[32,16,128]{2,1,0:T(8,128)S(1)}, u32[]{:S(2)}, u32[]{:S(2)}) %all-to-all-start) | async-done | bytes 262176 | tf_op jit(solution)/shard_map/all_to_all | solution.py:620
  24.2 2.4 %merge.1 = f32[16,16,128]{2,1,0:T(8,128)S(1)} custom-call(f32[32,16,128]{2,1,0:T(8,128)S(1)} %all-to-all-done.blocks_ref, bf16[10,256,256]{2,1,0:T(8,128)(2,1)S(1)} %get-tuple-element.9.weights_ref, f32[10,5,8,256]{3,2,1,0:T(8,128)S(1)} %get-tuple-element.10.waves_ref, f32[10,8,8,128]{3,2,1,0:T(8,128)S(1)} %get-tuple-element.11.taps_ref), custom_call_target="tpu_custom_call" | custom-call | flops 100000000 | bytes 1000000 | tf_op jit(solution)/shard_map/merge/pallas_call | solution.py:621
  26.6 22.7 %all_to_all.10 = f32[16,16,128]{2,1,0:T(8,128)S(1)} all-to-all(f32[16,16,128]{2,1,0:T(8,128)S(1)} %merge.1), channel_id=1, replica_groups=mesh['ap'=32,'pass'=16] {'pass'}, dimensions={0} | all-to-all | bytes 262144 | tf_op jit(solution)/shard_map/all_to_all | solution.py:639
  49.3 1.1 %invert.1 = f32[512,128]{1,0:T(8,128)} custom-call(f32[256,128]{1,0:T(8,128)S(1)} %bitcast.6, bf16[128,128]{1,0:T(8,128)(2,1)S(1)} %get-tuple-element.12.mixer_ref), custom_call_target="tpu_custom_call" | custom-call | flops 100000000 | bytes 1000000 | tf_op jit(solution)/shard_map/invert/pallas_call | solution.py:640
Async XLA Ops:
  4.0 20.2 %all-to-all-start = ((f32[32,16,128]{2,1,0:T(8,128)}), f32[32,16,128]{2,1,0:T(8,128)S(1)}, u32[]{:S(2)}, u32[]{:S(2)}) async-start(f32[32,16,128]{2,1,0:T(8,128)} %compress.1), calls=%async_computation | async-start | bytes 524288 | tf_op jit(solution)/shard_map/all_to_all | solution.py:620

commit v2 on v1

--- a/solution.py
+++ b/solution.py
@@ -13,6 +13,7 @@
 HEIGHTS = 64
 KT = 8
 ORIGIN = KT // 2 - 1
+RMAX = 16
 BASES = 32
 LEVELS = 8
 LOCAL = 3
@@ -21,6 +22,7 @@
 N_AP = 32
 PASSES = 16
 RW = 64
+QUARTERS = 4
 BEAMS = 256
 LANES = 128
 TILES = 17
@@ -114,6 +116,7 @@
     shifting,
     framed,
     images,
+    outgoing,
     *scalars,
 ):
     *tables, arrived = scalars
@@ -156,19 +159,7 @@
             previous = current
         bands.append(jnp.concatenate(pieces, axis=1))
     banded = jnp.concatenate(bands, axis=0)
-    for copy in fetch_tables:
-        copy.wait()
-
-    position = lax.axis_index("ap")
-    offset_above = jnp.int32(0)
-    for level in range(LOCAL, LEVELS):
-        bit = position // 2 ** (level - LOCAL) % 2
-        offset_above = offset_above + jnp.where(
-            bit == 1, step_offset(tables, level, 1), step_offset(tables, level, 0)
-        )
-    local_steps = [
-        [step_offset(tables, level, child) for child in range(2)] for level in range(LOCAL)
-    ]
+
     shifting[:, :8] = jnp.zeros((2 * PULSES, 8, LANES), F32)
     shifting[:, 8 + BLOCKS :] = jnp.zeros((2 * PULSES, 16, LANES), F32)
 
@@ -185,30 +176,21 @@
     for part in range(2):
         product[part] = correlated[:, part * LANES : (part + 1) * LANES]
 
-    for n in range(PULSES):
-        total = offset_above
-        for level in range(LOCAL):
-            total = total + local_steps[level][n >> level & 1]
-        whole = total >> 7
-        rest = total & (LANES - 1)
-        even, odd = (
-            [product[part, pl.ds(2 * n + i, BLOCKS, stride=16), :] for part in range(2)]
-            for i in range(2)
+    for copy in fetch_tables:
+        copy.wait()
+
+    position = lax.axis_index("ap")
+    offset_above = jnp.int32(0)
+    for level in range(LOCAL, LEVELS):
+        bit = position // 2 ** (level - LOCAL) % 2
+        offset_above = offset_above + jnp.where(
+            bit == 1, step_offset(tables, level, 1), step_offset(tables, level, 0)
         )
-        keep = iota((FRAME_ROWS, LANES), 1) < LANES - rest
-        for part, value in enumerate((even[0] + odd[1], odd[0] - even[1])):
-            i = 2 * n + part
-            shifting[i, 8 : 8 + BLOCKS] = pltpu.roll(value, (LANES - rest) & (LANES - 1), 1)
-            left = shifting[i, pl.ds(8 + whole, FRAME_ROWS), :]
-            right = shifting[i, pl.ds(9 + whole, FRAME_ROWS), :]
-            framed[i * FRAME_ROWS : (i + 1) * FRAME_ROWS] = jnp.where(keep, left, right)
-
-    def load(level, part, b):
-        if level == 0:
-            return framed[pl.ds(part * FRAME_ROWS + b, PULSES, stride=2 * FRAME_ROWS), :]
-        return images[level % 2, part, b]
-
-    for level in range(LOCAL):
+    local_steps = [
+        [step_offset(tables, level, child) for child in range(2)] for level in range(LOCAL)
+    ]
+
+    def prepare(level):
         beams = 2**level
         roles = [role(tables, level, child) for child in range(2)]
         in_child = rows8 >> level & 1
@@ -261,56 +243,118 @@
             waves.append((cos * SQRT_HALF, sin * SQRT_HALF))
             steps.append(sincos(slope * float(LANES)))
 
+        return tap_rows, left_side, cell_out, waves, steps
+
+    totals = []
+    for n in range(PULSES):
+        total = offset_above
+        for level in range(LOCAL):
+            total = total + local_steps[level][n >> level & 1]
+        totals.append(total)
+        rest = total & (LANES - 1)
+        even, odd = (
+            [product[part, pl.ds(2 * n + i, BLOCKS, stride=16), :] for part in range(2)]
+            for i in range(2)
+        )
+        for part, value in enumerate((even[0] + odd[1], odd[0] - even[1])):
+            shifting[2 * n + part, 8 : 8 + BLOCKS] = pltpu.roll(
+                value, (LANES - rest) & (LANES - 1), 1
+            )
+    lane = iota((FRAME_ROWS, LANES), 1)
+    for n in range(PULSES):
+        whole = totals[n] >> 7
+        keep = lane < LANES - (totals[n] & (LANES - 1))
+        for part in range(2):
+            i = 2 * n + part
+            left = shifting[i, pl.ds(8 + whole, FRAME_ROWS), :]
+            right = shifting[i, pl.ds(9 + whole, FRAME_ROWS), :]
+            framed[i * FRAME_ROWS : (i + 1) * FRAME_ROWS] = jnp.where(keep, left, right)
+
+    sends = []
+
+    def send(window, values):
+        block = reverse_bits(window)
+        for part in range(2):
+            outgoing[block % QUARTERS, block // QUARTERS, part * 8 : part * 8 + 8] = values[part]
+        if (window + 1) % (N_AP // QUARTERS) == 0:
+            quarter = block % QUARTERS
+            sends.append(
+                pltpu.make_async_copy(
+                    outgoing.at[quarter], out_ref.at[:, quarter], arrived.at[8 + quarter]
+                )
+            )
+            sends[-1].start()
+
+    def load(level, part, b):
+        if level == 0:
+            return framed[pl.ds(part * FRAME_ROWS + b, PULSES, stride=2 * FRAME_ROWS), :]
+        return images[level % 2, part, b]
+
+    for level in range(LOCAL):
+        tap_rows, left_side, cell_out, waves, steps = prepare(level)
+
+        def turn(value, cells):
+            return pltpu.roll(value, LANES - cells, 1)
+
+        def moved(here, there, cells):
+            return jnp.where(lanes8 < LANES - cells, here, there)
+
         def rolls(b):
+            values = [load(level, part, b) for part in range(2)]
+            return [[value] + [turn(value, u) for u in (1, 2, 3)] for value in values]
+
+        def runs(here, there):
             found = []
             for part in range(2):
-                value = load(level, part, b)
-                found.append([value] + [pltpu.roll(value, LANES - u, 1) for u in range(1, KT)])
+                value = here[part][0]
+                near, far = tap_rows[0] * value, tap_rows[4] * value
+                for u in (1, 2, 3):
+                    value = moved(here[part][u], there[part][u], u)
+                    near = near + tap_rows[u] * value
+                    far = far + tap_rows[4 + u] * value
+                found.append((near, turn(far, 4)))
             return found
 
         here = rolls(0)
+        there = rolls(1)
+        sums = runs(here, there)
         for b in range(TILES):
-            there = rolls(b + 1) if b + 1 < TILES else here
+            if b + 1 < TILES:
+                here, there = there, rolls(b + 2) if b + 2 < TILES else there
+                sums_there = runs(here, there)
             pieces = []
             for part in range(2):
-                total = tap_rows[0] * here[part][0]
-                for u in range(1, KT):
-                    moved = jnp.where(lanes8 < LANES - u, here[part][u], there[part][u])
-                    total = total + tap_rows[u] * moved
+                total = sums[part][0] + moved(sums[part][1], sums_there[part][1], 4)
                 high, low = split(total)
                 pieces.append(
                     jnp.concatenate([high, low, high, jnp.zeros((PULSES, LANES), F32)], axis=0)
                 )
+            sums = sums_there
             right_side = jnp.concatenate(pieces, axis=1).astype(BF16)
             steered = jnp.dot(left_side, right_side, preferred_element_type=F32)
-            out_real = jnp.zeros((PULSES, LANES), F32)
-            out_imag = jnp.zeros((PULSES, LANES), F32)
+            terms = []
             for child in range(2):
                 rows = steered[child * PULSES : (child + 1) * PULSES]
-                real, imag = complex_mul(*waves[child], rows[:, :LANES], rows[:, LANES:])
-                out_real = out_real + real
-                out_imag = out_imag + imag
+                terms.append(complex_mul(*waves[child], rows[:, :LANES], rows[:, LANES:]))
                 waves[child] = complex_mul(*waves[child], *steps[child])
-            where_r = cell_out + b * LANES
-            inside = (where_r >= 0) & (where_r < NR)
-            images[(level + 1) % 2, 0, b] = jnp.where(inside, out_real, 0.0)
-            images[(level + 1) % 2, 1, b] = jnp.where(inside, out_imag, 0.0)
-            here = there
-
-    last = LOCAL % 2
-    for block in range(N_AP):
-        start = reverse_bits(block) * RW
-        t = start // LANES
-        for part in range(2):
-            if start % LANES == 0:
-                value = images[last, part, t]
+            values = [a + c for a, c in zip(*terms)]
+            if b * LANES < LEVELS * (RMAX + ORIGIN) or (b + 1) * LANES > NR - LEVELS * RMAX:
+                where_r = cell_out + b * LANES
+                inside = (where_r >= 0) & (where_r < NR)
+                values = [jnp.where(inside, value, 0.0) for value in values]
+            if level + 1 < LOCAL:
+                for part in range(2):
+                    images[(level + 1) % 2, part, b] = values[part]
             else:
-                value = jnp.where(
-                    lanes8 < RW,
-                    pltpu.roll(images[last, part, t], RW, 1),
-                    pltpu.roll(images[last, part, t + 1], RW, 1),
-                )
-            out_ref[block, part * PULSES : (part + 1) * PULSES, :] = value
+                turned = [pltpu.roll(value, RW, 1) for value in values]
+                if b > 0:
+                    joined = [jnp.where(lanes8 < RW, a, c) for a, c in zip(before, turned)]
+                    send(2 * b - 1, joined)
+                if b < BLOCKS:
+                    send(2 * b, values)
+                before = turned
+    for copy in sends:
+        copy.wait()
 
 
 def column_offset(tables, level, column):
@@ -392,7 +436,7 @@
             cos, sin = sincos(jnp.broadcast_to(slope * 8.0, (8, 2 * LANES)))
             waves_ref[at, 2] = cos
             waves_ref[at, 3] = sin
-            waves_ref[at, 4] = cell.astype(F32)
+            waves_ref[at, 4] = cell.astype(F32) - (NR - 1) / 2
             for u in range(KT):
                 taps_ref[at, u] = jnp.full((8, LANES), range_taps_ref[level, e, u], F32)
 
@@ -423,31 +467,14 @@
 
 
 def merge_kernel(
-    blocks_ref,
-    weights_ref,
-    waves_ref,
-    taps_ref,
-    out_ref,
     blocks,
     weights,
     waves,
     taps,
+    out_ref,
     images,
     final,
-    arrived,
 ):
-    fetches = [pltpu.make_async_copy(blocks_ref, blocks, arrived.at[CROSS])]
-    fetches += [
-        pltpu.make_async_copy(
-            weights_ref.at[pl.ds(2 * k, 2)], weights.at[pl.ds(2 * k, 2)], arrived.at[k]
-        )
-        for k in range(CROSS)
-    ]
-    fetches.append(pltpu.make_async_copy(waves_ref, waves, arrived.at[CROSS + 1]))
-    fetches.append(pltpu.make_async_copy(taps_ref, taps, arrived.at[CROSS + 2]))
-    for fetch in fetches:
-        fetch.start()
-    fetches[0].wait()
     for child in range(2):
         order = []
         for i in range(N_AP // 2):
@@ -460,13 +487,10 @@
             )
             images[0, child, part] = stacked.T
 
-    fetches[CROSS + 1].wait()
-    fetches[CROSS + 2].wait()
     for k in range(CROSS):
         rows = ROWS[k]
         source, target = k % 2, 1 - k % 2
         last = k == CROSS - 1
-        fetches[1 + k].wait()
         steered = []
         for child in range(2):
             tap = [
@@ -492,23 +516,21 @@
         turning = [(waves[2 * k + child, 0], waves[2 * k + child, 1]) for child in range(2)]
         steps = [(waves[2 * k + child, 2], waves[2 * k + child, 3]) for child in range(2)]
         for m in range(rows // 8):
-            out_real = jnp.zeros((8, 2 * LANES), F32)
-            out_imag = jnp.zeros((8, 2 * LANES), F32)
+            terms = []
             for child in range(2):
-                real, imag = complex_mul(
-                    *turning[child],
-                    steered[child][8 * m : 8 * m + 8],
-                    steered[child][rows + 8 * m : rows + 8 * m + 8],
+                terms.append(
+                    complex_mul(
+                        *turning[child],
+                        steered[child][8 * m : 8 * m + 8],
+                        steered[child][rows + 8 * m : rows + 8 * m + 8],
+                    )
                 )
-                out_real = out_real + real
-                out_imag = out_imag + imag
                 turning[child] = complex_mul(*turning[child], *steps[child])
+            values = [a + c for a, c in zip(*terms)]
             if not last:
-                where_r = waves[2 * k, 4] + float(8 * m)
-                inside = (where_r >= 0) & (where_r < NR)
-                out_real = jnp.where(inside, out_real, 0.0)
-                out_imag = jnp.where(inside, out_imag, 0.0)
-            for part, value in enumerate((out_real, out_imag)):
+                inside = jnp.abs(waves[2 * k, 4] + float(8 * m)) < NR / 2
+                values = [jnp.where(inside, value, 0.0) for value in values]
+            for part, value in enumerate(values):
                 for side in range(2):
                     piece = value[:, side * LANES : (side + 1) * LANES]
                     if last:
@@ -531,11 +553,8 @@
                 out_ref[side * 8 + q, part * 8 : part * 8 + 8, :] = values[q]
 
 
-def invert_kernel(data_ref, mixer_ref, out_ref, data, arrived):
-    fetch = pltpu.make_async_copy(data_ref, data, arrived)
-    fetch.start()
+def invert_kernel(data, mixer_ref, out_ref):
     mixer = mixer_ref[...]
-    fetch.wait()
     for i in range(8):
         high, low = split(data[pl.ds(i, 2 * PASSES, stride=8), :])
         right_side = jnp.concatenate([high, low, high, jnp.zeros_like(high)], axis=0)
@@ -545,7 +564,6 @@
 
 
 VMEM = pl.BlockSpec(memory_space=pltpu.VMEM)
-ANY = pl.BlockSpec(memory_space=pl.ANY)
 HBM = pl.BlockSpec(memory_space=pltpu.HBM)
 LIMIT = 16 << 20
 
@@ -580,9 +598,9 @@
     blocks = pl.pallas_call(
         compress_kernel,
         name="compress",
-        out_shape=jax.ShapeDtypeStruct((N_AP, 2 * PULSES, LANES), F32),
+        out_shape=jax.ShapeDtypeStruct((N_AP // QUARTERS, QUARTERS, 2 * PULSES, LANES), F32),
         in_specs=[HBM] * 8,
-        out_specs=VMEM,
+        out_specs=HBM,
         scratch_shapes=[
             pltpu.VMEM((PULSES, 2, NS), BF16),
             pltpu.VMEM((2, TAPS), BF16),
@@ -591,8 +609,9 @@
             pltpu.VMEM((2 * PULSES, 24 + BLOCKS, LANES), F32),
             pltpu.VMEM((2 * PULSES * FRAME_ROWS, LANES), F32),
             pltpu.VMEM((2, 2, TILES, PULSES, LANES), F32),
+            pltpu.VMEM((QUARTERS, N_AP // QUARTERS, 2 * PULSES, LANES), F32),
             *held,
-            pltpu.SemaphoreType.DMA((8,)),
+            pltpu.SemaphoreType.DMA((8 + QUARTERS,)),
         ],
         compiler_params=params,
         cost_estimate=pl.CostEstimate(flops=10**8, bytes_accessed=10**6, transcendentals=0),
@@ -617,21 +636,17 @@
         compiler_params=params,
         cost_estimate=pl.CostEstimate(flops=10**8, bytes_accessed=10**6, transcendentals=0),
     )(*tables, in_hbm(jnp.transpose(invert, (0, 2, 1))), in_hbm(baseline_index))
+    blocks = blocks.reshape(N_AP, 2 * PULSES, LANES)
     blocks = lax.all_to_all(blocks, "ap", split_axis=0, concat_axis=0, tiled=True)
     stacks = pl.pallas_call(
         merge_kernel,
         name="merge",
         out_shape=jax.ShapeDtypeStruct((PASSES, 16, LANES), F32),
-        in_specs=[ANY] * 4,
+        in_specs=[VMEM] * 4,
         out_specs=VMEM,
         scratch_shapes=[
-            pltpu.VMEM((N_AP, 2 * PULSES, LANES), F32),
-            pltpu.VMEM((2 * CROSS, 2 * LANES, 2 * LANES), BF16),
-            pltpu.VMEM((2 * CROSS, 5, 8, 2 * LANES), F32),
-            pltpu.VMEM((2 * CROSS, KT, 8, LANES), F32),
             pltpu.VMEM((2, 2, 2, LANES, LANES), F32),
             pltpu.VMEM((2, 2, RW, LANES), F32),
-            pltpu.SemaphoreType.DMA((CROSS + 3,)),
         ],
         compiler_params=params,
         cost_estimate=pl.CostEstimate(flops=10**8, bytes_accessed=10**6, transcendentals=0),
@@ -641,9 +656,8 @@
         invert_kernel,
         name="invert",
         out_shape=jax.ShapeDtypeStruct((HEIGHTS * 8, LANES), F32),
-        in_specs=[ANY, VMEM],
+        in_specs=[VMEM, VMEM],
         out_specs=VMEM,
-        scratch_shapes=[pltpu.VMEM((PASSES * 16, LANES), F32), pltpu.SemaphoreType.DMA],
         compiler_params=params,
         cost_estimate=pl.CostEstimate(flops=10**8, bytes_accessed=10**6, transcendentals=0),
     )(stacks.reshape(PASSES * 16, LANES), mixer)

time: 50.8 us -> 49.4 us (0.972)
  Pallas kernels: 11.7 us -> 10.4 us
    pallas_call x1, Pallas kernels: 2.44 us -> 1.75 us  [body(): pl.pallas_call(merge_kernel, name='merge', out_shape=jax.ShapeDtypeStruct...]
  transfers between devices with their start and end apart: 1 -> 1, of which waited for: 1 -> 1; matrix products, arithmetic and copies ran while one was open for 0% -> 0% of each run, Pallas kernels for 8% -> 9%
where the time goes in v2:
time: 49.4 us; the launch traced here: 49.1 us
  blocking collectives  22.7 us (46%)
  starting transfers between devices  10.5 us (21%)
  Pallas kernels  10.4 us (21%)
  waiting for transfers between devices  5.47 us (11%)
    all_to_all x1, blocking collectives, body(): lax.all_to_all(stacks, 'pass', split_axis=0, concat_axis=0, tiled=True)  22.7 us
    all_to_all x1, starting transfers between devices, body(): lax.all_to_all(blocks, 'ap', split_axis=0, concat_axis=0, tiled=True)  10.5 us
    all_to_all x1, waiting for transfers between devices, body(): lax.all_to_all(blocks, 'ap', split_axis=0, concat_axis=0, tiled=True)  5.47 us
    pallas_call x1, Pallas kernels, body(): pl.pallas_call(tables_kernel, name='tables', out_shape=(jax.ShapeDtypeStr...  4.21 us
    pallas_call x1, Pallas kernels, body(): pl.pallas_call(compress_kernel, name='compress', out_shape=jax.ShapeDtype...  3.48 us
    pallas_call x1, Pallas kernels, body(): pl.pallas_call(merge_kernel, name='merge', out_shape=jax.ShapeDtypeStruct...  1.75 us
  transfers between devices with their start and end apart: 1, of which 1 were waited for; matrix products, arithmetic and copies ran while one was open for 0% of the time, Pallas kernels for 9%

profile of v2, /device:TPU:1, one launch (start us, length us, event | category | flops | bytes accessed | tf_op | source)
XLA Modules:
  0.0 49.1 jit_solution(15842651973110993570)
XLA Ops:
  0.0 3.5 %compress.1 = f32[8,4,16,128]{3,2,1,0:T(8,128)} custom-call(bf16[1,8,2,3072]{3,2,1,0:T(2,128)(2,1)} %echo_ref.1, bf16[2,1024]{1,0:T(2,128)(2,1)} %chirp_ref.1, s32[1,8]{1,0:T(1,128)} %swap_ref.3, s32[1,2,8]{2,1,0:T(2,128)} %bitcast.12, s32[1,2,2,8]{3,2,1,0:T(2,128)} %bitcast.10, f32[8,2,8]{2,1,0:T(2,128)} %range_taps_ref.3, f32[8,2,2,8]{3,2,1,0:T(2,128)} %angle_taps_ref.3, ...), custom_call_target="tpu_custom_call" | custom-call | flops 100000000 | bytes 1000000 | tf_op jit(solution)/shard_map/compress/pallas_call | solution.py:598
  3.5 10.5 %all-to-all-start = ((f32[32,16,128]{2,1,0:T(8,128)}), f32[32,16,128]{2,1,0:T(8,128)S(1)}, u32[]{:S(2)}, u32[]{:S(2)}) async-start(f32[32,16,128]{2,1,0:T(8,128)} %bitcast.3), calls=%async_computation | async-start | bytes 524288 | tf_op jit(solution)/shard_map/all_to_all | solution.py:640
  14.0 4.2 %tables.1 = (bf16[10,256,256]{2,1,0:T(8,128)(2,1)S(1)}, f32[10,5,8,256]{3,2,1,0:T(8,128)S(1)}, f32[10,8,8,128]{3,2,1,0:T(8,128)S(1)}, bf16[128,128]{1,0:T(8,128)(2,1)S(1)}) custom-call(s32[1,8]{1,0:T(1,128)} %swap_ref.3, s32[1,2,8]{2,1,0:T(2,128)} %bitcast.13, s32[1,2,2,8]{3,2,1,0:T(2,128)} %bitcast.11, f32[8,2,8]{2,1,0:T(2,128)} %range_taps_ref.3, ...), custom_call_target="tpu_custom_call" | custom-call | flops 100000000 | bytes 1000000 | tf_op jit(solution)/shard_map/tables/pallas_call | solution.py:619
  18.2 5.5 %all-to-all-done.blocks = f32[32,16,128]{2,1,0:T(8,128)S(1)} async-done(((f32[32,16,128]{2,1,0:T(8,128)}), f32[32,16,128]{2,1,0:T(8,128)S(1)}, u32[]{:S(2)}, u32[]{:S(2)}) %all-to-all-start) | async-done | bytes 262176 | tf_op jit(solution)/shard_map/all_to_all | solution.py:640
  23.7 1.8 %merge.1 = f32[16,16,128]{2,1,0:T(8,128)S(1)} custom-call(f32[32,16,128]{2,1,0:T(8,128)S(1)} %all-to-all-done.blocks, bf16[10,256,256]{2,1,0:T(8,128)(2,1)S(1)} %get-tuple-element.9.weights, f32[10,5,8,256]{3,2,1,0:T(8,128)S(1)} %get-tuple-element.10.waves, f32[10,8,8,128]{3,2,1,0:T(8,128)S(1)} %get-tuple-element.11.taps), custom_call_target="tpu_custom_call" | custom-call | flops 100000000 | bytes 1000000 | tf_op jit(solution)/shard_map/merge/pallas_call | solution.py:641
  25.4 22.7 %all_to_all.10 = f32[16,16,128]{2,1,0:T(8,128)S(1)} all-to-all(f32[16,16,128]{2,1,0:T(8,128)S(1)} %merge.1), channel_id=1, replica_groups=mesh['ap'=32,'pass'=16] {'pass'}, dimensions={0} | all-to-all | bytes 262144 | tf_op jit(solution)/shard_map/all_to_all | solution.py:654
  48.2 0.9 %invert.1 = f32[512,128]{1,0:T(8,128)} custom-call(f32[256,128]{1,0:T(8,128)S(1)} %bitcast.7, bf16[128,128]{1,0:T(8,128)(2,1)S(1)} %get-tuple-element.12.mixer_ref), custom_call_target="tpu_custom_call" | custom-call | flops 100000000 | bytes 1000000 | tf_op jit(solution)/shard_map/invert/pallas_call | solution.py:655
Async XLA Ops:
  3.5 20.2 %all-to-all-start = ((f32[32,16,128]{2,1,0:T(8,128)}), f32[32,16,128]{2,1,0:T(8,128)S(1)}, u32[]{:S(2)}, u32[]{:S(2)}) async-start(f32[32,16,128]{2,1,0:T(8,128)} %bitcast.3), calls=%async_computation | async-start | bytes 524288 | tf_op jit(solution)/shard_map/all_to_all | solution.py:640

commit v3 on v2

--- a/solution.py
+++ b/solution.py
@@ -34,6 +34,7 @@
 BF16 = jnp.bfloat16
 
 ROWS = (96, 88, 80, 72, 64)
+FIRST_ROW = tuple(sum(ROWS[:k]) for k in range(CROSS))
 
 
 def iota(shape, dim):
@@ -408,11 +409,13 @@
     parity = column & 1
     for k in range(CROSS):
         level = LOCAL + k
+        first_wave = FIRST_ROW[k]
         beams = 2**level
         beam = column % (2 * beams) // 2
         first_row = column // (2 * beams) * beams
         beam_fraction = (column % (2 * beams)).astype(F32) / (2.0 * beams)
         cell = iota((8, 2 * LANES), 0) + (base + column_offset(tables, level, column))
+        centred = cell.astype(F32) - (NR - 1) / 2
         for child in range(2):
             e = role(tables, level, child)
             shift = jnp.where(
@@ -431,14 +434,17 @@
             weights_ref[at, LANES:] = low.astype(BF16)
             slope, bend = slope_and_bend(tables, level, e, parity)
             cos, sin = sincos(slope * cell.astype(F32) + bend * beam_fraction)
-            waves_ref[at, 0] = cos * SQRT_HALF
-            waves_ref[at, 1] = sin * SQRT_HALF
-            cos, sin = sincos(jnp.broadcast_to(slope * 8.0, (8, 2 * LANES)))
-            waves_ref[at, 2] = cos
-            waves_ref[at, 3] = sin
-            waves_ref[at, 4] = cell.astype(F32) - (NR - 1) / 2
+            wave = (cos * SQRT_HALF, sin * SQRT_HALF)
+            step = sincos(jnp.broadcast_to(slope * 8.0, (8, 2 * LANES)))
+            for m in range(ROWS[k] // 8):
+                inside = jnp.abs(centred + float(8 * m)) < NR / 2
+                for part in range(2):
+                    waves_ref[child, part, first_wave + 8 * m : first_wave + 8 * m + 8] = (
+                        jnp.where(inside, wave[part], 0.0)
+                    )
+                wave = complex_mul(*wave, *step)
             for u in range(KT):
-                taps_ref[at, u] = jnp.full((8, LANES), range_taps_ref[level, e, u], F32)
+                taps_ref[at, u : u + 1] = jnp.full((1, LANES), range_taps_ref[level, e, u], F32)
 
     lane = iota((1, LANES), 1)
     wanted = jnp.zeros((1, LANES), jnp.int32)
@@ -494,7 +500,7 @@
         steered = []
         for child in range(2):
             tap = [
-                jnp.concatenate([taps[2 * k + child, u]] * (rows // 8), axis=0) for u in range(KT)
+                jnp.broadcast_to(taps[2 * k + child, u : u + 1], (rows, LANES)) for u in range(KT)
             ]
             parts = []
             for part in range(2):
@@ -513,23 +519,18 @@
                     preferred_element_type=F32,
                 )
             )
-        turning = [(waves[2 * k + child, 0], waves[2 * k + child, 1]) for child in range(2)]
-        steps = [(waves[2 * k + child, 2], waves[2 * k + child, 3]) for child in range(2)]
         for m in range(rows // 8):
-            terms = []
-            for child in range(2):
-                terms.append(
-                    complex_mul(
-                        *turning[child],
-                        steered[child][8 * m : 8 * m + 8],
-                        steered[child][rows + 8 * m : rows + 8 * m + 8],
-                    )
+            at = FIRST_ROW[k] + 8 * m
+            terms = [
+                complex_mul(
+                    waves[child, 0, at : at + 8],
+                    waves[child, 1, at : at + 8],
+                    steered[child][8 * m : 8 * m + 8],
+                    steered[child][rows + 8 * m : rows + 8 * m + 8],
                 )
-                turning[child] = complex_mul(*turning[child], *steps[child])
+                for child in range(2)
+            ]
             values = [a + c for a, c in zip(*terms)]
-            if not last:
-                inside = jnp.abs(waves[2 * k, 4] + float(8 * m)) < NR / 2
-                values = [jnp.where(inside, value, 0.0) for value in values]
             for part, value in enumerate(values):
                 for side in range(2):
                     piece = value[:, side * LANES : (side + 1) * LANES]
@@ -621,8 +622,8 @@
         name="tables",
         out_shape=(
             jax.ShapeDtypeStruct((2 * CROSS, 2 * LANES, 2 * LANES), BF16),
-            jax.ShapeDtypeStruct((2 * CROSS, 5, 8, 2 * LANES), F32),
-            jax.ShapeDtypeStruct((2 * CROSS, KT, 8, LANES), F32),
+            jax.ShapeDtypeStruct((2, 2, sum(ROWS), 2 * LANES), F32),
+            jax.ShapeDtypeStruct((2 * CROSS, KT, LANES), F32),
             jax.ShapeDtypeStruct((2 * HEIGHTS, LANES), BF16),
         ),
         in_specs=[HBM] * 8,

time: 49.4 us -> 49.4 us (level)
  no operation moved by 1% of the time
where the time goes in v3:
time: 49.4 us; the launch traced here: 49 us
  blocking collectives  22.7 us (46%)
  Pallas kernels  10.6 us (21%)
  starting transfers between devices  10.5 us (21%)
  waiting for transfers between devices  5.2 us (11%)
    all_to_all x1, blocking collectives, body(): lax.all_to_all(stacks, 'pass', split_axis=0, concat_axis=0, tiled=True)  22.7 us
    all_to_all x1, starting transfers between devices, body(): lax.all_to_all(blocks, 'ap', split_axis=0, concat_axis=0, tiled=True)  10.5 us
    all_to_all x1, waiting for transfers between devices, body(): lax.all_to_all(blocks, 'ap', split_axis=0, concat_axis=0, tiled=True)  5.2 us
    pallas_call x1, Pallas kernels, body(): pl.pallas_call(tables_kernel, name='tables', out_shape=(jax.ShapeDtypeStr...  4.47 us
    pallas_call x1, Pallas kernels, body(): pl.pallas_call(compress_kernel, name='compress', out_shape=jax.ShapeDtype...  3.48 us
    pallas_call x1, Pallas kernels, body(): pl.pallas_call(merge_kernel, name='merge', out_shape=jax.ShapeDtypeStruct...  1.72 us
  transfers between devices with their start and end apart: 1, of which 1 were waited for; matrix products, arithmetic and copies ran while one was open for 0% of the time, Pallas kernels for 9%

profile of v3, /device:TPU:1, one launch (start us, length us, event | category | flops | bytes accessed | tf_op | source)
XLA Modules:
  0.0 49.0 jit_solution(12013262816082650110)
XLA Ops:
  0.0 3.5 %compress.1 = f32[8,4,16,128]{3,2,1,0:T(8,128)} custom-call(bf16[1,8,2,3072]{3,2,1,0:T(2,128)(2,1)} %echo_ref.1, bf16[2,1024]{1,0:T(2,128)(2,1)} %chirp_ref.1, s32[1,8]{1,0:T(1,128)} %swap_ref.3, s32[1,2,8]{2,1,0:T(2,128)} %bitcast.12, s32[1,2,2,8]{3,2,1,0:T(2,128)} %bitcast.10, f32[8,2,8]{2,1,0:T(2,128)} %range_taps_ref.3, f32[8,2,2,8]{3,2,1,0:T(2,128)} %angle_taps_ref.3, ...), custom_call_target="tpu_custom_call" | custom-call | flops 100000000 | bytes 1000000 | tf_op jit(solution)/shard_map/compress/pallas_call | solution.py:599
  3.5 10.5 %all-to-all-start = ((f32[32,16,128]{2,1,0:T(8,128)}), f32[32,16,128]{2,1,0:T(8,128)S(1)}, u32[]{:S(2)}, u32[]{:S(2)}) async-start(f32[32,16,128]{2,1,0:T(8,128)} %bitcast.3), calls=%async_computation | async-start | bytes 524288 | tf_op jit(solution)/shard_map/all_to_all | solution.py:641
  14.0 4.5 %tables.1 = (bf16[10,256,256]{2,1,0:T(8,128)(2,1)S(1)}, f32[2,2,400,256]{3,2,1,0:T(8,128)S(1)}, f32[10,8,128]{2,1,0:T(8,128)S(1)}, bf16[128,128]{1,0:T(8,128)(2,1)S(1)}) custom-call(s32[1,8]{1,0:T(1,128)} %swap_ref.3, s32[1,2,8]{2,1,0:T(2,128)} %bitcast.13, s32[1,2,2,8]{3,2,1,0:T(2,128)} %bitcast.11, f32[8,2,8]{2,1,0:T(2,128)} %range_taps_ref.3, ...), custom_call_target="tpu_custom_call" | custom-call | flops 100000000 | bytes 1000000 | tf_op jit(solution)/shard_map/tables/pallas_call | solution.py:620
  18.5 5.2 %all-to-all-done.blocks = f32[32,16,128]{2,1,0:T(8,128)S(1)} async-done(((f32[32,16,128]{2,1,0:T(8,128)}), f32[32,16,128]{2,1,0:T(8,128)S(1)}, u32[]{:S(2)}, u32[]{:S(2)}) %all-to-all-start) | async-done | bytes 262176 | tf_op jit(solution)/shard_map/all_to_all | solution.py:641
  23.7 1.7 %merge.1 = f32[16,16,128]{2,1,0:T(8,128)S(1)} custom-call(f32[32,16,128]{2,1,0:T(8,128)S(1)} %all-to-all-done.blocks, bf16[10,256,256]{2,1,0:T(8,128)(2,1)S(1)} %get-tuple-element.9.weights, f32[2,2,400,256]{3,2,1,0:T(8,128)S(1)} %get-tuple-element.10.waves, f32[10,8,128]{2,1,0:T(8,128)S(1)} %get-tuple-element.11.taps), custom_call_target="tpu_custom_call" | custom-call | flops 100000000 | bytes 1000000 | tf_op jit(solution)/shard_map/merge/pallas_call | solution.py:642
  25.4 22.7 %all_to_all.10 = f32[16,16,128]{2,1,0:T(8,128)S(1)} all-to-all(f32[16,16,128]{2,1,0:T(8,128)S(1)} %merge.1), channel_id=1, replica_groups=mesh['ap'=32,'pass'=16] {'pass'}, dimensions={0} | all-to-all | bytes 262144 | tf_op jit(solution)/shard_map/all_to_all | solution.py:655
  48.1 0.9 %invert.1 = f32[512,128]{1,0:T(8,128)} custom-call(f32[256,128]{1,0:T(8,128)S(1)} %bitcast.7, bf16[128,128]{1,0:T(8,128)(2,1)S(1)} %get-tuple-element.12.mixer_ref), custom_call_target="tpu_custom_call" | custom-call | flops 100000000 | bytes 1000000 | tf_op jit(solution)/shard_map/invert/pallas_call | solution.py:656
Async XLA Ops:
  3.5 20.2 %all-to-all-start = ((f32[32,16,128]{2,1,0:T(8,128)}), f32[32,16,128]{2,1,0:T(8,128)S(1)}, u32[]{:S(2)}, u32[]{:S(2)}) async-start(f32[32,16,128]{2,1,0:T(8,128)} %bitcast.3), calls=%async_computation | async-start | bytes 524288 | tf_op jit(solution)/shard_map/all_to_all | solution.py:641

commit v4 on v2

--- a/solution.py
+++ b/solution.py
@@ -23,6 +23,8 @@
 PASSES = 16
 RW = 64
 QUARTERS = 4
+AP_FIRST = 20
+PASS_FIRST = 12
 BEAMS = 256
 LANES = 128
 TILES = 17
@@ -273,7 +275,7 @@
     sends = []
 
     def send(window, values):
-        block = reverse_bits(window)
+        block = reverse_bits(window) ^ AP_FIRST
         for part in range(2):
             outgoing[block % QUARTERS, block // QUARTERS, part * 8 : part * 8 + 8] = values[part]
         if (window + 1) % (N_AP // QUARTERS) == 0:
@@ -443,7 +445,7 @@
     lane = iota((1, LANES), 1)
     wanted = jnp.zeros((1, LANES), jnp.int32)
     for p in range(PASSES):
-        wanted = jnp.where(lane % (2 * PASSES) // 2 == p, baseline[p], wanted)
+        wanted = jnp.where(lane % (2 * PASSES) // 2 == p ^ PASS_FIRST, baseline[p], wanted)
     chosen = (iota((BASES, LANES), 0) == wanted).astype(F32)
     steer = [
         lax.dot_general(
@@ -483,7 +485,7 @@
             )
         for part in range(2):
             stacked = jnp.concatenate(
-                [blocks[g, part * PULSES : (part + 1) * PULSES, :] for g in order], axis=0
+                [blocks[g ^ AP_FIRST, part * PULSES : (part + 1) * PULSES, :] for g in order], axis=0
             )
             images[0, child, part] = stacked.T
 
@@ -550,7 +552,8 @@
                         values[i] = jnp.where(clear, a, pltpu.roll(b, 16 * d, 1))
                         values[i | d] = jnp.where(clear, pltpu.roll(a, LANES - 16 * d, 1), b)
             for q in range(8):
-                out_ref[side * 8 + q, part * 8 : part * 8 + 8, :] = values[q]
+                at = (side * 8 + q) ^ PASS_FIRST
+                out_ref[at, part * 8 : part * 8 + 8, :] = values[q]
 
 
 def invert_kernel(data, mixer_ref, out_ref):
@@ -566,6 +569,11 @@
 VMEM = pl.BlockSpec(memory_space=pltpu.VMEM)
 HBM = pl.BlockSpec(memory_space=pltpu.HBM)
 LIMIT = 16 << 20
+
+
+def exchange(array, axis, first):
+    members = [i ^ first for i in range(lax.axis_size(axis))]
+    return lax.all_to_all(array, axis, 0, 0, axis_index_groups=[members], tiled=True)
 
 
 def in_hbm(array):
@@ -637,7 +645,7 @@
         cost_estimate=pl.CostEstimate(flops=10**8, bytes_accessed=10**6, transcendentals=0),
     )(*tables, in_hbm(jnp.transpose(invert, (0, 2, 1))), in_hbm(baseline_index))
     blocks = blocks.reshape(N_AP, 2 * PULSES, LANES)
-    blocks = lax.all_to_all(blocks, "ap", split_axis=0, concat_axis=0, tiled=True)
+    blocks = exchange(blocks, "ap", AP_FIRST)
     stacks = pl.pallas_call(
         merge_kernel,
         name="merge",
@@ -651,7 +659,7 @@
         compiler_params=params,
         cost_estimate=pl.CostEstimate(flops=10**8, bytes_accessed=10**6, transcendentals=0),
     )(blocks, weights, waves, taps)
-    stacks = lax.all_to_all(stacks, "pass", split_axis=0, concat_axis=0, tiled=True)
+    stacks = exchange(stacks, "pass", PASS_FIRST)
     power = pl.pallas_call(
         invert_kernel,
         name="invert",

time: 49.4 us -> 43.4 us (0.88)
  waiting for transfers between devices: 5.47 us -> 0.01 us
  blocking collectives: 22.7 us -> 20.1 us
  starting transfers between devices: 10.5 us -> 12.5 us
    all_to_all x1, waiting for transfers between devices: 5.47 us -> 0.01 us  [exchange(): lax.all_to_all(array, axis, 0, 0, axis_index_groups=[members], tiled=True)]
    all_to_all x1, blocking collectives: 22.7 us -> 20.1 us  [exchange(): lax.all_to_all(array, axis, 0, 0, axis_index_groups=[members], tiled=True)]
    all_to_all x1, starting transfers between devices: 10.5 us -> 12.5 us  [exchange(): lax.all_to_all(array, axis, 0, 0, axis_index_groups=[members], tiled=True)]
  transfers between devices with their start and end apart: 1 -> 1, of which waited for: 1 -> 0; matrix products, arithmetic and copies ran while one was open for 0% -> 0% of each run, Pallas kernels for 9% -> 10%
where the time goes in v4:
time: 43.4 us; the launch traced here: 43 us
  blocking collectives  20.1 us (46%)
  starting transfers between devices  12.5 us (29%)
  Pallas kernels  10.4 us (24%)
    all_to_all x1, blocking collectives, exchange(): lax.all_to_all(array, axis, 0, 0, axis_index_groups=[members], tiled=True)  20.1 us
    all_to_all x1, starting transfers between devices, exchange(): lax.all_to_all(array, axis, 0, 0, axis_index_groups=[members], tiled=True)  12.5 us
    pallas_call x1, Pallas kernels, body(): pl.pallas_call(tables_kernel, name='tables', out_shape=(jax.ShapeDtypeStr...  4.21 us
    pallas_call x1, Pallas kernels, body(): pl.pallas_call(compress_kernel, name='compress', out_shape=jax.ShapeDtype...  3.48 us
    pallas_call x1, Pallas kernels, body(): pl.pallas_call(merge_kernel, name='merge', out_shape=jax.ShapeDtypeStruct...  1.75 us
    pallas_call x1, Pallas kernels, body(): pl.pallas_call(invert_kernel, name='invert', out_shape=jax.ShapeDtypeStru...  0.93 us
  transfers between devices with their start and end apart: 1, of which 0 were waited for; matrix products, arithmetic and copies ran while one was open for 0% of the time, Pallas kernels for 10%

profile of v4, /device:TPU:1, one launch (start us, length us, event | category | flops | bytes accessed | tf_op | source)
XLA Modules:
  0.0 43.0 jit_solution(2524196084209153181)
XLA Ops:
  0.0 3.5 %compress.1 = f32[8,4,16,128]{3,2,1,0:T(8,128)} custom-call(bf16[1,8,2,3072]{3,2,1,0:T(2,128)(2,1)} %echo_ref.1, bf16[2,1024]{1,0:T(2,128)(2,1)} %chirp_ref.1, s32[1,8]{1,0:T(1,128)} %swap_ref.3, s32[1,2,8]{2,1,0:T(2,128)} %bitcast.12, s32[1,2,2,8]{3,2,1,0:T(2,128)} %bitcast.10, f32[8,2,8]{2,1,0:T(2,128)} %range_taps_ref.3, f32[8,2,2,8]{3,2,1,0:T(2,128)} %angle_taps_ref.3, ...), custom_call_target="tpu_custom_call" | custom-call | flops 100000000 | bytes 1000000 | tf_op jit(solution)/shard_map/compress/pallas_call | solution.py:606
  3.5 12.5 %all-to-all-start = ((f32[32,16,128]{2,1,0:T(8,128)}), f32[32,16,128]{2,1,0:T(8,128)S(1)}, u32[]{:S(2)}, u32[]{:S(2)}) async-start(f32[32,16,128]{2,1,0:T(8,128)} %bitcast.3), calls=%async_computation | async-start | bytes 524288 | tf_op jit(solution)/shard_map/all_to_all | solution.py:576
  16.0 4.2 %tables.1 = (bf16[10,256,256]{2,1,0:T(8,128)(2,1)S(1)}, f32[10,5,8,256]{3,2,1,0:T(8,128)S(1)}, f32[10,8,8,128]{3,2,1,0:T(8,128)S(1)}, bf16[128,128]{1,0:T(8,128)(2,1)S(1)}) custom-call(s32[1,8]{1,0:T(1,128)} %swap_ref.3, s32[1,2,8]{2,1,0:T(2,128)} %bitcast.13, s32[1,2,2,8]{3,2,1,0:T(2,128)} %bitcast.11, f32[8,2,8]{2,1,0:T(2,128)} %range_taps_ref.3, ...), custom_call_target="tpu_custom_call" | custom-call | flops 100000000 | bytes 1000000 | tf_op jit(solution)/shard_map/tables/pallas_call | solution.py:627
  20.2 0.0 all-to-all-done.blocks
  20.2 1.8 %merge.1 = f32[16,16,128]{2,1,0:T(8,128)S(1)} custom-call(f32[32,16,128]{2,1,0:T(8,128)S(1)} %all-to-all-done.blocks, bf16[10,256,256]{2,1,0:T(8,128)(2,1)S(1)} %get-tuple-element.9.weights, f32[10,5,8,256]{3,2,1,0:T(8,128)S(1)} %get-tuple-element.10.waves, f32[10,8,8,128]{3,2,1,0:T(8,128)S(1)} %get-tuple-element.11.taps), custom_call_target="tpu_custom_call" | custom-call | flops 100000000 | bytes 1000000 | tf_op jit(solution)/shard_map/merge/pallas_call | solution.py:649
  22.0 20.1 %all_to_all.10 = f32[16,16,128]{2,1,0:T(8,128)S(1)} all-to-all(f32[16,16,128]{2,1,0:T(8,128)S(1)} %merge.1), channel_id=1, replica_groups={{12,13,14,15,8,9,10,11,4,5,6,7,0,1,2,3},{28,29,30,31,24,25,26,27,20,21,..., dimensions={0} | all-to-all | bytes 262144 | tf_op jit(solution)/shard_map/all_to_all | solution.py:576
  42.1 0.9 %invert.1 = f32[512,128]{1,0:T(8,128)} custom-call(f32[256,128]{1,0:T(8,128)S(1)} %bitcast.7, bf16[128,128]{1,0:T(8,128)(2,1)S(1)} %get-tuple-element.12.mixer_ref), custom_call_target="tpu_custom_call" | custom-call | flops 100000000 | bytes 1000000 | tf_op jit(solution)/shard_map/invert/pallas_call | solution.py:663
Async XLA Ops:
  3.5 16.7 %all-to-all-start = ((f32[32,16,128]{2,1,0:T(8,128)}), f32[32,16,128]{2,1,0:T(8,128)S(1)}, u32[]{:S(2)}, u32[]{:S(2)}) async-start(f32[32,16,128]{2,1,0:T(8,128)} %bitcast.3), calls=%async_computation | async-start | bytes 524288 | tf_op jit(solution)/shard_map/all_to_all | solution.py:576

commit v5 on v3

--- a/solution.py
+++ b/solution.py
@@ -23,6 +23,8 @@
 PASSES = 16
 RW = 64
 QUARTERS = 4
+AP_FIRST = 20
+PASS_FIRST = 12
 BEAMS = 256
 LANES = 128
 TILES = 17
@@ -274,7 +276,7 @@
     sends = []
 
     def send(window, values):
-        block = reverse_bits(window)
+        block = reverse_bits(window) ^ AP_FIRST
         for part in range(2):
             outgoing[block % QUARTERS, block // QUARTERS, part * 8 : part * 8 + 8] = values[part]
         if (window + 1) % (N_AP // QUARTERS) == 0:
@@ -449,7 +451,7 @@
     lane = iota((1, LANES), 1)
     wanted = jnp.zeros((1, LANES), jnp.int32)
     for p in range(PASSES):
-        wanted = jnp.where(lane % (2 * PASSES) // 2 == p, baseline[p], wanted)
+        wanted = jnp.where(lane % (2 * PASSES) // 2 == p ^ PASS_FIRST, baseline[p], wanted)
     chosen = (iota((BASES, LANES), 0) == wanted).astype(F32)
     steer = [
         lax.dot_general(
@@ -489,7 +491,7 @@
             )
         for part in range(2):
             stacked = jnp.concatenate(
-                [blocks[g, part * PULSES : (part + 1) * PULSES, :] for g in order], axis=0
+                [blocks[g ^ AP_FIRST, part * PULSES : (part + 1) * PULSES, :] for g in order], axis=0
             )
             images[0, child, part] = stacked.T
 
@@ -551,7 +553,8 @@
                         values[i] = jnp.where(clear, a, pltpu.roll(b, 16 * d, 1))
                         values[i | d] = jnp.where(clear, pltpu.roll(a, LANES - 16 * d, 1), b)
             for q in range(8):
-                out_ref[side * 8 + q, part * 8 : part * 8 + 8, :] = values[q]
+                at = (side * 8 + q) ^ PASS_FIRST
+                out_ref[at, part * 8 : part * 8 + 8, :] = values[q]
 
 
 def invert_kernel(data, mixer_ref, out_ref):
@@ -567,6 +570,11 @@
 VMEM = pl.BlockSpec(memory_space=pltpu.VMEM)
 HBM = pl.BlockSpec(memory_space=pltpu.HBM)
 LIMIT = 16 << 20
+
+
+def exchange(array, axis, first):
+    members = [i ^ first for i in range(lax.axis_size(axis))]
+    return lax.all_to_all(array, axis, 0, 0, axis_index_groups=[members], tiled=True)
 
 
 def in_hbm(array):
@@ -638,7 +646,7 @@
         cost_estimate=pl.CostEstimate(flops=10**8, bytes_accessed=10**6, transcendentals=0),
     )(*tables, in_hbm(jnp.transpose(invert, (0, 2, 1))), in_hbm(baseline_index))
     blocks = blocks.reshape(N_AP, 2 * PULSES, LANES)
-    blocks = lax.all_to_all(blocks, "ap", split_axis=0, concat_axis=0, tiled=True)
+    blocks = exchange(blocks, "ap", AP_FIRST)
     stacks = pl.pallas_call(
         merge_kernel,
         name="merge",
@@ -652,7 +660,7 @@
         compiler_params=params,
         cost_estimate=pl.CostEstimate(flops=10**8, bytes_accessed=10**6, transcendentals=0),
     )(blocks, weights, waves, taps)
-    stacks = lax.all_to_all(stacks, "pass", split_axis=0, concat_axis=0, tiled=True)
+    stacks = exchange(stacks, "pass", PASS_FIRST)
     power = pl.pallas_call(
         invert_kernel,
         name="invert",

time: 49.4 us -> 43.3 us (0.88)
  waiting for transfers between devices: 5.2 us -> 0.01 us
  blocking collectives: 22.7 us -> 19.9 us
  starting transfers between devices: 10.5 us -> 12.5 us
    all_to_all x1, waiting for transfers between devices: 5.2 us -> 0.01 us  [exchange(): lax.all_to_all(array, axis, 0, 0, axis_index_groups=[members], tiled=True)]
    all_to_all x1, blocking collectives: 22.7 us -> 19.9 us  [exchange(): lax.all_to_all(array, axis, 0, 0, axis_index_groups=[members], tiled=True)]
    all_to_all x1, starting transfers between devices: 10.5 us -> 12.5 us  [exchange(): lax.all_to_all(array, axis, 0, 0, axis_index_groups=[members], tiled=True)]
  transfers between devices with their start and end apart: 1 -> 1, of which waited for: 1 -> 0; matrix products, arithmetic and copies ran while one was open for 0% -> 0% of each run, Pallas kernels for 9% -> 10%
where the time goes in v5:
time: 43.3 us; the launch traced here: 43 us
  blocking collectives  19.9 us (46%)
  starting transfers between devices  12.5 us (29%)
  Pallas kernels  10.6 us (24%)
    all_to_all x1, blocking collectives, exchange(): lax.all_to_all(array, axis, 0, 0, axis_index_groups=[members], tiled=True)  19.9 us
    all_to_all x1, starting transfers between devices, exchange(): lax.all_to_all(array, axis, 0, 0, axis_index_groups=[members], tiled=True)  12.5 us
    pallas_call x1, Pallas kernels, body(): pl.pallas_call(tables_kernel, name='tables', out_shape=(jax.ShapeDtypeStr...  4.47 us
    pallas_call x1, Pallas kernels, body(): pl.pallas_call(compress_kernel, name='compress', out_shape=jax.ShapeDtype...  3.48 us
    pallas_call x1, Pallas kernels, body(): pl.pallas_call(merge_kernel, name='merge', out_shape=jax.ShapeDtypeStruct...  1.73 us
    pallas_call x1, Pallas kernels, body(): pl.pallas_call(invert_kernel, name='invert', out_shape=jax.ShapeDtypeStru...  0.92 us
  transfers between devices with their start and end apart: 1, of which 0 were waited for; matrix products, arithmetic and copies ran while one was open for 0% of the time, Pallas kernels for 10%

profile of v5, /device:TPU:1, one launch (start us, length us, event | category | flops | bytes accessed | tf_op | source)
XLA Modules:
  0.0 43.0 jit_solution(14141121435118595285)
XLA Ops:
  0.0 3.5 %compress.1 = f32[8,4,16,128]{3,2,1,0:T(8,128)} custom-call(bf16[1,8,2,3072]{3,2,1,0:T(2,128)(2,1)} %echo_ref.1, bf16[2,1024]{1,0:T(2,128)(2,1)} %chirp_ref.1, s32[1,8]{1,0:T(1,128)} %swap_ref.3, s32[1,2,8]{2,1,0:T(2,128)} %bitcast.12, s32[1,2,2,8]{3,2,1,0:T(2,128)} %bitcast.10, f32[8,2,8]{2,1,0:T(2,128)} %range_taps_ref.3, f32[8,2,2,8]{3,2,1,0:T(2,128)} %angle_taps_ref.3, ...), custom_call_target="tpu_custom_call" | custom-call | flops 100000000 | bytes 1000000 | tf_op jit(solution)/shard_map/compress/pallas_call | solution.py:607
  3.5 12.5 %all-to-all-start = ((f32[32,16,128]{2,1,0:T(8,128)}), f32[32,16,128]{2,1,0:T(8,128)S(1)}, u32[]{:S(2)}, u32[]{:S(2)}) async-start(f32[32,16,128]{2,1,0:T(8,128)} %bitcast.3), calls=%async_computation | async-start | bytes 524288 | tf_op jit(solution)/shard_map/all_to_all | solution.py:577
  16.0 4.5 %tables.1 = (bf16[10,256,256]{2,1,0:T(8,128)(2,1)S(1)}, f32[2,2,400,256]{3,2,1,0:T(8,128)S(1)}, f32[10,8,128]{2,1,0:T(8,128)S(1)}, bf16[128,128]{1,0:T(8,128)(2,1)S(1)}) custom-call(s32[1,8]{1,0:T(1,128)} %swap_ref.3, s32[1,2,8]{2,1,0:T(2,128)} %bitcast.13, s32[1,2,2,8]{3,2,1,0:T(2,128)} %bitcast.11, f32[8,2,8]{2,1,0:T(2,128)} %range_taps_ref.3, ...), custom_call_target="tpu_custom_call" | custom-call | flops 100000000 | bytes 1000000 | tf_op jit(solution)/shard_map/tables/pallas_call | solution.py:628
  20.5 0.0 all-to-all-done.blocks
  20.5 1.7 %merge.1 = f32[16,16,128]{2,1,0:T(8,128)S(1)} custom-call(f32[32,16,128]{2,1,0:T(8,128)S(1)} %all-to-all-done.blocks, bf16[10,256,256]{2,1,0:T(8,128)(2,1)S(1)} %get-tuple-element.9.weights, f32[2,2,400,256]{3,2,1,0:T(8,128)S(1)} %get-tuple-element.10.waves, f32[10,8,128]{2,1,0:T(8,128)S(1)} %get-tuple-element.11.taps), custom_call_target="tpu_custom_call" | custom-call | flops 100000000 | bytes 1000000 | tf_op jit(solution)/shard_map/merge/pallas_call | solution.py:650
  22.2 19.9 %all_to_all.10 = f32[16,16,128]{2,1,0:T(8,128)S(1)} all-to-all(f32[16,16,128]{2,1,0:T(8,128)S(1)} %merge.1), channel_id=1, replica_groups={{12,13,14,15,8,9,10,11,4,5,6,7,0,1,2,3},{28,29,30,31,24,25,26,27,20,21,..., dimensions={0} | all-to-all | bytes 262144 | tf_op jit(solution)/shard_map/all_to_all | solution.py:577
  42.1 0.9 %invert.1 = f32[512,128]{1,0:T(8,128)} custom-call(f32[256,128]{1,0:T(8,128)S(1)} %bitcast.7, bf16[128,128]{1,0:T(8,128)(2,1)S(1)} %get-tuple-element.12.mixer_ref), custom_call_target="tpu_custom_call" | custom-call | flops 100000000 | bytes 1000000 | tf_op jit(solution)/shard_map/invert/pallas_call | solution.py:664
Async XLA Ops:
  3.5 17.0 %all-to-all-start = ((f32[32,16,128]{2,1,0:T(8,128)}), f32[32,16,128]{2,1,0:T(8,128)S(1)}, u32[]{:S(2)}, u32[]{:S(2)}) async-start(f32[32,16,128]{2,1,0:T(8,128)} %bitcast.3), calls=%async_computation | async-start | bytes 524288 | tf_op jit(solution)/shard_map/all_to_all | solution.py:577
